TPU v7x, 32 devices: a whole 2x2x4 slice. The times are simulated.
32 devices in a mesh: groups: 2 (over x), tensor: 16 (over z, y, core).
Axes of the slice: x: 2, y: 2, z: 4, core: 2. Of those that a mesh axis runs over, the one named last changes fastest.
Arguments:
- span_rows: bfloat16 [32, 8192], P(('groups', 'tensor')), parts along dimension 0, may hold values from -6 to 6
- decode_rows: bfloat16 [2, 32, 8192], P(None, ('groups', 'tensor')), parts along dimension 1, may hold values from -6 to 6
- norm_gain: bfloat16 [8192], replicated, may hold values from 0.099609375 to 1.8984375
- w_query: bfloat16 [8192, 8192], P(None, 'tensor'), may hold values from -0.0625 to 0.0625
- w_keyval: bfloat16 [8192, 2048], P(None, 'tensor'), may hold values from -0.0625 to 0.0625
- prefix_keys: bfloat16 [8192, 1024], P(('groups', 'tensor')), parts along dimension 0, may hold values from -304 to 304
- prefix_values: bfloat16 [8192, 1024], P(('groups', 'tensor')), parts along dimension 0, may hold values from -6 to 6
- span_offset: int32 [2], P('groups'), parts along dimension 0, may hold values from 2048 to 4096
- pool_keys: bfloat16 [1024, 16, 1024], P(('groups', 'tensor')), parts along dimension 0, may hold values from -304 to 304
- pool_values: bfloat16 [1024, 16, 1024], P(('groups', 'tensor')), parts along dimension 0, may hold values from -6 to 6
- row_blocks: int32 [32, 32], P('groups'), parts along dimension 0, may hold values from 0 to 511, as said below
- context_lens: int32 [32], P('groups'), parts along dimension 0, may hold values from 1 to 512, 4096 in all
Outputs:
- span_attended: bfloat16 [32, 8192], P(('groups', 'tensor')), parts along dimension 0
- decode_attended: bfloat16 [2, 32, 8192], P(None, ('groups', 'tensor')), parts along dimension 1
- span_cache: bfloat16 [32, 2048], P(('groups', 'tensor')), parts along dimension 0
There are 2 independent parts, one for each index of `groups`. A program takes and returns all parts, laid end to end along the dimension named above; an argument that names none is the same for every part. Nothing has to cross between parts.
Inputs may be any that keep to these rules, and one draw needn't show every extreme that they name: Prefix slots from span_offset on are unused. `row_blocks`: every cache block belongs to exactly one decode row; entry k of a row holds its positions k * 16 to k * 16 + 15. `context_lens`: some row has exactly 512 cached tokens.
All inputs are finite; a program needn't handle non-finite values.
Results may differ from a plain program's by a relative error of at most 0.0065.
The roundings to bfloat16 on the way count: a program that leaves them out, or rounds other values in their place, can miss the bound.
Values may be sent and summed in bfloat16 or wider, within the bound.
A program may use at most 128 MiB of HBM per device.

v0:
```python
import math

import jax
import jax.numpy as jnp
import numpy as np
from jax import lax
from jax.sharding import PartitionSpec as P

D = 8192
H = 64
KVH = 8
HD = 128
PAGE = 16
STEPS = 2
BLK_ROW = 32


epsilon = 1e-05
neg_fill = -1e30
rotation_bits = 20


def normalize(row_block, gain_vector):
    widened = row_block.astype(jnp.float32)
    mean_square = jnp.mean(widened * widened, axis=-1, keepdims=True)
    return (widened * lax.rsqrt(mean_square + epsilon) * gain_vector.astype(jnp.float32)).astype(
        jnp.bfloat16
    )


def llama_frequencies(half_width):
    exponents = np.arange(half_width) / (1.0 * half_width)
    inverse = 1.0 / 500000.0**exponents
    wavelen = 2.0 * np.pi / inverse
    scaled = np.where(wavelen > 8192.0, inverse / 8.0, inverse)
    smooth = (8192.0 / wavelen - 1.0) / 3.0
    blended = (1.0 - smooth) * inverse / 8.0 + smooth * inverse
    middle = (wavelen >= 2048.0) & (wavelen <= 8192.0)
    return np.where(middle, blended, scaled)


def rotation_tables(half_width):
    frequencies = llama_frequencies(half_width)
    powers = 2.0 ** np.arange(rotation_bits)
    angles = powers[:, None] * frequencies[None, :]
    return (jnp.asarray(np.cos(angles), jnp.float32), jnp.asarray(np.sin(angles), jnp.float32))


def rotate(projected, positions, head_count):
    row_count = projected.shape[0]
    half_width = HD // 2
    cos_table, sin_table = rotation_tables(half_width)
    cos_part = jnp.ones((row_count, half_width), jnp.float32)
    sin_part = jnp.zeros((row_count, half_width), jnp.float32)
    for bit_index in range(rotation_bits):
        chosen = (positions >> bit_index & 1).astype(jnp.float32)[:, None]
        step_cos = 1.0 + chosen * (cos_table[bit_index] - 1.0)
        step_sin = chosen * sin_table[bit_index]
        cos_part, sin_part = (
            cos_part * step_cos - sin_part * step_sin,
            sin_part * step_cos + cos_part * step_sin,
        )
    shaped = projected.astype(jnp.float32).reshape(row_count, head_count, HD)
    first_half = shaped[..., :half_width]
    second_half = shaped[..., half_width:]
    cos_part = cos_part[:, None, :]
    sin_part = sin_part[:, None, :]
    turned = jnp.concatenate(
        [
            first_half * cos_part - second_half * sin_part,
            second_half * cos_part + first_half * sin_part,
        ],
        axis=-1,
    )
    return turned.reshape(row_count, head_count * HD).astype(jnp.bfloat16)


def shards(
    span_rows,
    decode_rows,
    norm_gain,
    w_query,
    w_keyval,
    prefix_keys,
    prefix_values,
    span_offset,
    pool_keys,
    pool_values,
    row_blocks,
    context_lens,
):
    devices = lax.axis_size("tensor")
    my_rank = lax.axis_index("tensor")
    span_dev = span_rows.shape[0]
    rows_dev = decode_rows.shape[1]
    local_count = span_dev + STEPS * rows_dev
    group_size = H // KVH
    kv_width = KVH * HD
    score_scale = 1.0 / math.sqrt(HD)
    offset = span_offset[0]
    row_total = context_lens.shape[0]
    span_total = span_dev * devices
    query_cols = w_query.shape[1]
    local_rows = jnp.concatenate([span_rows, decode_rows.reshape(STEPS * rows_dev, D)], axis=0)
    normed = normalize(local_rows, norm_gain)
    shard_rows = lax.all_gather(normed, "tensor", axis=0, tiled=True)
    queries = jnp.dot(shard_rows, w_query, preferred_element_type=jnp.float32)
    keyval = jnp.dot(shard_rows, w_keyval, preferred_element_type=jnp.float32)
    projected = jnp.concatenate([queries, keyval], axis=1).astype(jnp.bfloat16)
    query_part = projected[:, :query_cols]
    keyval_part = projected[:, query_cols:]
    device_ids = jnp.arange(devices, dtype=jnp.int32)[:, None]
    local_ids = jnp.arange(local_count, dtype=jnp.int32)[None, :]
    span_positions = offset + device_ids * span_dev + local_ids
    decode_local = jnp.maximum(local_ids - span_dev, 0)
    owner_rows = device_ids * rows_dev + decode_local % rows_dev
    decode_positions = jnp.take(context_lens, owner_rows) + decode_local // rows_dev
    positions = jnp.where(local_ids < span_dev, span_positions, decode_positions)
    my_positions = lax.dynamic_index_in_dim(positions, my_rank, 0, keepdims=False)
    queries_full, keyval_full = (
        lax.all_gather(query_part, "tensor", axis=1, tiled=True),
        lax.all_gather(keyval_part, "tensor", axis=1, tiled=True),
    )
    keyval_own = lax.dynamic_slice_in_dim(keyval_full, my_rank * local_count, local_count, 0)
    queries_rot = rotate(queries_full, positions.reshape(-1), H).reshape(devices, local_count, D)
    keys_own = rotate(keyval_own[:, :kv_width], my_positions, KVH)
    values_own = keyval_own[:, kv_width:]
    span_cache = jnp.concatenate([keys_own[:span_dev], values_own[:span_dev]], axis=1)
    span_queries = queries_rot[:, :span_dev].reshape(span_total, KVH, group_size, HD)
    local_keys = jnp.concatenate([prefix_keys, keys_own[:span_dev]], axis=0).reshape(-1, KVH, HD)
    local_values = jnp.concatenate([prefix_values, values_own[:span_dev]], axis=0).reshape(
        -1, KVH, HD
    )
    prefix_dev = prefix_keys.shape[0]
    slot_ids = jnp.arange(prefix_dev + span_dev, dtype=jnp.int32)
    prefix_pos = my_rank * prefix_dev + slot_ids
    span_token = my_rank * span_dev + slot_ids - prefix_dev
    query_ids = jnp.arange(span_total, dtype=jnp.int32)[:, None]
    allowed = jnp.where(
        slot_ids[None, :] < prefix_dev,
        (prefix_pos < offset)[None, :],
        span_token[None, :] <= query_ids,
    )
    span_scores = (
        jnp.einsum("igqd,kgd->igqk", span_queries, local_keys, preferred_element_type=jnp.float32)
        * score_scale
    )
    span_scores = jnp.where(allowed[:, None, None, :], span_scores, neg_fill)
    span_peak = jnp.max(span_scores, axis=-1)
    block_dev = pool_keys.shape[0]
    block_ids = my_rank * block_dev + jnp.arange(block_dev, dtype=jnp.int32)
    flat_map = row_blocks.reshape(-1)
    entry_ids = jnp.arange(flat_map.shape[0], dtype=jnp.int32)
    found_at = jnp.sum(
        jnp.where(flat_map[None, :] == block_ids[:, None], entry_ids[None, :], 0), axis=1
    )
    block_rows = found_at // BLK_ROW
    block_slots = found_at % BLK_ROW
    token_pos = block_slots[:, None] * PAGE + jnp.arange(PAGE, dtype=jnp.int32)[None, :]
    live_tokens = token_pos < jnp.take(context_lens, block_rows)[:, None]
    decode_queries = (
        queries_rot[:, span_dev:]
        .reshape(devices, STEPS, rows_dev, D)
        .transpose(0, 2, 1, 3)
        .reshape(row_total, STEPS, D)
    )
    block_queries = jnp.take(decode_queries, block_rows, axis=0).reshape(
        block_dev, STEPS, KVH, group_size, HD
    )
    block_keys = pool_keys.reshape(block_dev, PAGE, KVH, HD)
    block_scores = (
        jnp.einsum(
            "bsgqd,bugd->bsgqu", block_queries, block_keys, preferred_element_type=jnp.float32
        )
        * score_scale
    )
    block_scores = jnp.where(live_tokens[:, None, None, None, :], block_scores, neg_fill)
    block_peak = jnp.max(block_scores, axis=-1)
    member = block_rows[:, None] == jnp.arange(row_total, dtype=jnp.int32)[None, :]
    row_peak = jnp.max(
        jnp.where(member[:, :, None, None, None], block_peak[:, None], neg_fill), axis=0
    )
    own_start = my_rank * rows_dev
    own_queries = lax.dynamic_slice_in_dim(decode_queries, own_start, rows_dev, 0).reshape(
        rows_dev, STEPS, KVH, group_size, HD
    )
    new_keys = keys_own[span_dev:].reshape(STEPS, rows_dev, KVH, HD)
    new_values = values_own[span_dev:].reshape(STEPS, rows_dev, KVH, HD)
    new_scores = (
        jnp.einsum("rsgqd,trgd->rsgqt", own_queries, new_keys, preferred_element_type=jnp.float32)
        * score_scale
    )
    step_ids = jnp.arange(STEPS, dtype=jnp.int32)
    causal = (step_ids[None, :] <= step_ids[:, None])[None, :, None, None, :]
    new_scores = jnp.where(causal, new_scores, neg_fill)
    own_peak = lax.dynamic_slice_in_dim(row_peak, own_start, rows_dev, 0)
    row_peak = lax.dynamic_update_slice_in_dim(
        row_peak, jnp.maximum(own_peak, jnp.max(new_scores, axis=-1)), own_start, 0
    )
    span_top, row_top = lax.pmax((span_peak, row_peak), "tensor")
    span_weights = jnp.where(
        allowed[:, None, None, :], jnp.exp(span_scores - span_top[..., None]), 0.0
    )
    span_den = jnp.sum(span_weights, axis=-1).reshape(span_total, H)
    span_num = jnp.einsum(
        "igqk,kgd->igqd",
        span_weights.astype(jnp.bfloat16),
        local_values,
        preferred_element_type=jnp.float32,
    ).reshape(span_total, D)
    block_top = jnp.take(row_top, block_rows, axis=0)
    block_weights = jnp.where(
        live_tokens[:, None, None, None, :], jnp.exp(block_scores - block_top[..., None]), 0.0
    )
    block_den = jnp.sum(block_weights, axis=-1).reshape(block_dev, STEPS * H)
    block_values = pool_values.reshape(block_dev, PAGE, KVH, HD)
    block_num = jnp.einsum(
        "bsgqu,bugd->bsgqd",
        block_weights.astype(jnp.bfloat16),
        block_values,
        preferred_element_type=jnp.float32,
    ).reshape(block_dev, STEPS * D)
    member_wide = member.astype(jnp.float32).T
    row_num = jnp.dot(member_wide, block_num, precision=lax.Precision.HIGHEST)
    row_den = jnp.dot(member_wide, block_den, precision=lax.Precision.HIGHEST)
    own_top = lax.dynamic_slice_in_dim(row_top, own_start, rows_dev, 0)
    new_weights = jnp.where(causal, jnp.exp(new_scores - own_top[..., None]), 0.0)
    new_den = jnp.sum(new_weights, axis=-1).reshape(rows_dev, STEPS * H)
    new_num = jnp.einsum(
        "rsgqt,trgd->rsgqd",
        new_weights.astype(jnp.bfloat16),
        new_values,
        preferred_element_type=jnp.float32,
    ).reshape(rows_dev, STEPS * D)
    row_num = lax.dynamic_update_slice_in_dim(
        row_num, lax.dynamic_slice_in_dim(row_num, own_start, rows_dev, 0) + new_num, own_start, 0
    )
    row_den = lax.dynamic_update_slice_in_dim(
        row_den, lax.dynamic_slice_in_dim(row_den, own_start, rows_dev, 0) + new_den, own_start, 0
    )
    row_num, row_den = (row_num, row_den)
    span_sum, span_weight, row_sum, row_weight = (
        lax.psum_scatter(span_num, "tensor", scatter_dimension=0, tiled=True),
        lax.psum_scatter(span_den, "tensor", scatter_dimension=0, tiled=True),
        lax.psum_scatter(row_num, "tensor", scatter_dimension=0, tiled=True),
        lax.psum_scatter(row_den, "tensor", scatter_dimension=0, tiled=True),
    )
    span_attended = (
        (span_sum.reshape(span_dev, H, HD) / span_weight.reshape(span_dev, H, 1))
        .reshape(span_dev, D)
        .astype(jnp.bfloat16)
    )
    decode_attended = (
        row_sum.reshape(rows_dev, STEPS, H, HD) / row_weight.reshape(rows_dev, STEPS, H, 1)
    ).astype(jnp.bfloat16)
    decode_attended = decode_attended.reshape(rows_dev, STEPS, D).transpose(1, 0, 2)
    return (span_attended, decode_attended, span_cache)


def solution(mesh):
    in_specs = (
        P(("groups", "tensor"), None),
        P(None, ("groups", "tensor"), None),
        P(),
        P(None, "tensor"),
        P(None, "tensor"),
        P(("groups", "tensor"), None),
        P(("groups", "tensor"), None),
        P("groups"),
        P(("groups", "tensor"), None, None),
        P(("groups", "tensor"), None, None),
        P("groups", None),
        P("groups"),
    )
    out_specs = (
        P(("groups", "tensor"), None),
        P(None, ("groups", "tensor"), None),
        P(("groups", "tensor"), None),
    )
    return jax.shard_map(shards, mesh=mesh, in_specs=in_specs, out_specs=out_specs, check_vma=False)
```

profile of v0, /device:TPU:13, one launch (start us, length us, event | category | flops | bytes accessed | tf_op | source)
XLA Modules:
  0.0 290.6 jit_solution(13363861140586934568)
XLA Ops:
  8.9 0.8 gather_fusion
  10.1 1.0 fusion.73
  11.1 1.0 fusion.72
  12.2 0.9 fusion.125
  13.2 0.9 fusion.124
  14.1 0.2 fusion.29
  14.3 0.1 fusion.32
  14.5 21.5 %all-gather = bf16[16,3,8192]{2,1,0:T(4,128)(2,1)} all-gather(bf16[1,3,8192]{2,1,0:T(4,128)(2,1)S(1)} %fusion.32), channel_id=1, replica_groups=mesh['groups'=2,'tensor'=16] {'tensor'}, dimensions={0}, use_global_device_ids=true | all-gather | bytes 835584 | tf_op jit(solution)/shard_map/all_gather | solution.py:106
  35.9 1.7 reshape.5311
  37.7 4.9 %convolution_convert_fusion = bf16[48,512]{1,0:T(8,128)(2,1)S(1)} fusion(bf16[48,8192]{1,0:T(8,128)(2,1)S(1)} %reshape.5311, bf16[8192,512]{1,0:T(8,128)(2,1)} %param.19), kind=kOutput, calls=%fused_computation.23 | convolution fusion | flops 402677760 | bytes 9224192 | tf_op jit(solution)/shard_map/dot_general | solution.py:107
  42.6 22.1 %all_gather.11 = bf16[48,8192]{1,0:T(8,128)(2,1)S(1)} all-gather(bf16[48,512]{1,0:T(8,128)(2,1)S(1)} %convolution_convert_fusion), channel_id=1, replica_groups=mesh['groups'=2,'tensor'=16] {'tensor'}, dimensions={1}, use_global_device_ids=true | all-gather | bytes 835584 | tf_op jit(solution)/shard_map/all_gather | solution.py:121
  64.7 0.1 convert_bitcast_fusion
  64.8 0.3 copy.118
  65.1 0.7 subtract_convert_fusion
  65.8 1.3 pad_maximum_fusion
  67.2 3.3 %convert_element_type.449 = bf16[16,3,8192]{2,1,0:T(4,128)(2,1)} reshape(bf16[48,64,128]{2,1,0:T(8,128)(2,1)} %pad_maximum_fusion) | data formatting | bytes 1572864 | tf_op jit(solution)/shard_map/convert_element_type | solution.py:75
  70.4 3.3 %slice_reduce_fusion = bf16[16,8192]{1,0:T(8,128)(2,1)} fusion(bf16[16,3,8192]{2,1,0:T(4,128)(2,1)} %convert_element_type.449), kind=kLoop, calls=%fused_computation.54 | loop fusion | bytes 524288 | tf_op jit(solution)/shard_map/slice | solution.py:129
  73.8 1.8 slice.397
  75.7 0.2 select_reduce_fusion.1
  75.9 0.7 gather_fusion.1
  76.6 3.6 %gather_fusion.2 = bf16[32,2,8192]{2,1,0:T(2,128)(2,1)} fusion(bf16[16,2,8192]{2,1,0:T(2,128)(2,1)S(1)} %slice.397, s32[1024]{0:T(1024)S(1)} %pad_clamp_fusion), kind=kCustom, calls=%fused_computation.2 | custom fusion | bytes 2097280 | tf_op jit(solution)/shard_map/jit(_take)/gather | solution.py:167
  80.3 1.7 copy.119
  82.0 0.5 convolution_convert_fusion.1
  82.5 18.1 %all_gather.10 = bf16[48,2048]{1,0:T(8,128)(2,1)S(1)} all-gather(bf16[48,128]{1,0:T(8,128)(2,1)S(1)} %convolution_convert_fusion.1), channel_id=1, replica_groups=mesh['groups'=2,'tensor'=16] {'tensor'}, dimensions={1}, use_global_device_ids=true | all-gather | bytes 208896 | tf_op jit(solution)/shard_map/all_gather | solution.py:122
  101.0 0.8 slice_bitcast_fusion
  101.9 1.6 copy.121
  103.4 1.1 bitcast_bitcast_fusion.1
  104.5 1.6 reshape.5318
  106.2 3.8 %bitcast_reduce_fusion = (f32[32,2,8,8]{3,1,2,0:T(2,128)S(1)}, f32[32,8,2,8,16]{4,3,2,1,0:T(8,128)}) fusion(pred[32,16]{1,0:T(8,128)(4,1)S(1)} %add_compare_fusion, bf16[32,16,8,128,1]{3,2,1,0,4:T(8,128)(2,1)} %bitcast_bitcast_fusion.1, bf16[32,2,8,8,128]{4,3,2,1,0:T(8,128)(2,1)} %reshape.5318, pred[32]{0:T(512)(128)(4,1)S(1)} %get-tuple-element.10), kind=kOutput, calls=%fused_computation.8 | convolution fusion | flops 17494016 | bytes 2376224 | tf_op jit(solution)/shard_map/bsgqd,bugd->bsgqu/dot_general | solution.py:172
  110.0 0.2 copy.88
  110.2 0.3 select_reduce_fusion
  110.6 0.3 fusion.142
  110.9 1.6 fusion.141
  112.6 48.4 %all-reduce.6 = (f32[16,8,8]{0,2,1:T(8,128)S(1)}, f32[16,2,8,8]{3,2,1,0:T(8,128)S(1)}) all-reduce(f32[16,8,8]{0,2,1:T(8,128)S(1)} %get-tuple-element.59, f32[16,2,8,8]{3,2,1,0:T(8,128)S(1)} %fusion.77), channel_id=1, replica_groups=mesh['groups'=2,'tensor'=16] {'tensor'}, use_global_device_ids=true, to_apply=%region_2.3 | all-reduce | flops 3072 | bytes 24576 | tf_op jit(solution)/shard_map/pmax | solution.py:200
  161.0 0.6 gather_fusion.3
  161.7 0.1 copy.91
  161.9 0.9 dynamic-slice.8
  163.0 0.3 copy-done.2
  163.3 0.5 convolution_bitcast_fusion.1
  163.7 0.2 copy.84
  163.9 1.1 copy.161
  165.0 0.3 copy.123
  165.3 0.1 bitcast_bitcast_fusion
  165.4 1.2 copy-done.5
  166.6 1.3 convolution_bitcast_fusion
  168.0 0.3 copy.93
  168.2 2.0 fusion
  170.3 1.1 convolution_bitcast_fusion.2
  171.4 0.5 dynamic_update_slice.10
  171.9 1.0 copy-done.3
  172.9 2.7 fusion.5
  175.7 0.1 fusion.133
  175.8 0.2 copy.97
  176.0 0.1 fusion.79
  176.3 0.6 dynamic-slice
  176.9 1.9 fusion.7
  178.8 59.0 %all-reduce.4 = (f32[16,64]{0,1:T(8,128)S(1)}, f32[16,128]{1,0:T(8,128)S(1)}) all-reduce(f32[16,64]{0,1:T(8,128)S(1)} %bitcast.195, f32[16,128]{1,0:T(8,128)S(1)} %dynamic_update_slice.11), channel_id=3, replica_groups=mesh['groups'=2,'tensor'=16] {'tensor'}, use_global_device_ids=true, to_apply=%region_5.6.clone | all-reduce | flops 3072 | bytes 24576
  237.8 0.7 fusion.126
  238.6 0.8 dynamic-slice_reduce_fusion.1
  239.5 0.6 pad_maximum_fusion.4
  240.1 38.7 %all-reduce.9.cloned.1.call-done = (f32[16,8192]{1,0:T(8,128)}, f32[16,16384]{1,0:T(8,128)}) async-done(((f32[16,8192]{1,0:T(8,128)}, f32[16,16384]{1,0:T(8,128)}), (f32[16,8192]{1,0:T(8,128)}, f32[16,16384]{1,0:T(8,128)})) %all-reduce.9.cloned.1.call-update) | async-done | bytes 1572880
  278.8 1.9 dynamic-slice_reduce_fusion
  280.8 2.3 fusion.34
  283.0 0.7 divide_convert_fusion
  (161 shorter events, 2.4 us)
Async XLA Ops:
  7.2 74.8 %copy-start = (bf16[8192,128]{1,0:T(8,128)(2,1)S(1)}, bf16[8192,128]{1,0:T(8,128)(2,1)}, u32[]{:S(2)}) copy-start(bf16[8192,128]{1,0:T(8,128)(2,1)} %param.20) | copy-start | bytes 6291460
  7.2 1.2 copy-start.1
  7.2 271.6 %all-reduce.9.cloned.1.call-start = ((), (), s32[]{:S(2)}) async-start(), calls=%async_computation | async-start | bytes 3145728
  8.4 1.3 copy-start.15
  8.4 1.3 copy-start.16
  8.4 1.3 copy-start.17
  8.5 1.3 copy-start.18
  8.5 1.3 copy-start.19
  8.5 1.3 copy-start.20
  8.5 1.3 copy-start.21
  8.5 1.3 copy-start.22
  8.5 1.3 copy-start.23
  8.5 1.3 copy-start.24
  8.5 1.3 copy-start.25
  8.6 1.3 copy-start.26
  8.6 1.3 copy-start.27
  8.6 1.3 copy-start.28
  8.6 1.3 copy-start.29
  8.6 1.3 copy-start.30
  8.6 1.3 copy-start.31
  8.6 1.2 copy-start.32
  8.6 1.2 copy-start.33
  8.7 1.2 copy-start.34
  8.7 1.2 copy-start.35
  8.7 1.2 copy-start.36
  8.7 1.2 copy-start.37
  8.7 1.2 copy-start.38
  8.7 1.2 copy-start.39
  8.7 1.2 copy-start.40
  8.7 1.2 copy-start.41
  8.8 1.2 copy-start.42
  8.8 1.2 copy-start.43
  8.8 1.2 copy-start.44
  8.8 1.2 copy-start.45
  8.8 1.2 copy-start.46
  8.8 1.2 copy-start.47
  8.8 1.2 copy-start.48
  8.8 1.2 copy-start.49
  8.9 5.2 %copy-start.14 = (bf16[8192]{0:T(1024)(128)(2,1)S(1)}, bf16[8192]{0:T(1024)(128)(2,1)}, u32[]{:S(2)}) copy-start(bf16[8192]{0:T(1024)(128)(2,1)} %param.18) | copy-start | bytes 49156
  8.9 5.2 %copy-start.12 = (bf16[2,1,8192]{2,0,1:T(2,128)(2,1)S(1)}, bf16[2,1,8192]{2,0,1:T(2,128)(2,1)}, u32[]{:S(2)}) copy-start(bf16[2,1,8192]{2,0,1:T(2,128)(2,1)} %param.17) | copy-start | bytes 98308
  8.9 5.2 %copy-start.13 = (bf16[1,8192]{1,0:T(2,128)(2,1)S(1)}, bf16[1,8192]{1,0:T(2,128)(2,1)}, u32[]{:S(2)}) copy-start(bf16[1,8192]{1,0:T(2,128)(2,1)} %param.16) | copy-start | bytes 49156
  67.1 8.5 %copy-start.50 = (s32[16,32]{1,0:T(8,128)S(1)}, s32[16,32]{1,0:T(8,128)}, u32[]{:S(2)}) copy-start(s32[16,32]{1,0:T(8,128)} %param.26) | copy-start | bytes 6148
  75.6 34.9 %copy-start.51 = (pred[2,2]{1,0:T(4,128)(4,1)}, pred[2,2]{1,0:T(4,128)(4,1)S(1)}, u32[]{:S(2)}) copy-start(pred[2,2]{1,0:T(4,128)(4,1)S(1)} %iota_compare_fusion.5) | copy-start | bytes 16
  80.2 20.6 %copy-start.8 = (bf16[256,1024]{1,0:T(8,128)(2,1)S(1)}, bf16[256,1024]{1,0:T(8,128)(2,1)}, u32[]{:S(2)}) copy-start(bf16[256,1024]{1,0:T(8,128)(2,1)} %param.21) | copy-start | bytes 1572868
  100.6 1.2 copy-start.11
  101.8 2.7 copy-start.4
  106.2 4.8 %copy-start.7 = (bf16[257,8,128,1]{2,1,0,3:T(8,128)(2,1)S(1)}, bf16[257,8,128,1]{2,1,0,3:T(8,128)(2,1)}, u32[]{:S(2)}) copy-start(bf16[257,8,128,1]{2,1,0,3:T(8,128)(2,1)} %slice_bitcast_fusion) | copy-start | bytes 1579012
  106.2 4.8 %copy-start.10 = (bf16[2,8,64,128]{3,2,1,0:T(8,128)(2,1)S(1)}, bf16[2,8,64,128]{3,2,1,0:T(8,128)(2,1)}, u32[]{:S(2)}) copy-start(bf16[2,8,64,128]{3,2,1,0:T(8,128)(2,1)} %copy.119) | copy-start | bytes 786436
  112.6 50.2 %copy-start.9 = (bf16[256,1024]{1,0:T(8,128)(2,1)S(1)}, bf16[256,1024]{1,0:T(8,128)(2,1)}, u32[]{:S(2)}) copy-start(bf16[256,1024]{1,0:T(8,128)(2,1)} %param.22) | copy-start | bytes 1572868
  161.8 1.4 copy-start.2
  163.3 1.8 copy-start.6
  165.0 1.6 copy-start.5
  171.9 1.0 copy-start.3
  171.9 3.7 %copy-start.52 = (pred[2,2]{1,0:T(4,128)(4,1)S(1)}, pred[2,2]{1,0:T(4,128)(4,1)}, u32[]{:S(2)}) copy-start(pred[2,2]{1,0:T(4,128)(4,1)} %copy-done.51) | copy-start | bytes 16
  171.9 4.4 %copy-start.53 = (u32[32]{0:T(128)S(1)}, u32[32]{0:T(128)}, u32[]{:S(2)}) copy-start(u32[32]{0:T(128)} %constant.358) | copy-start | bytes 388
Sparse Core Ops, SparseCore 0:
  173.1 105.6 all-reduce.8
where the time goes:
time: 295 us; the launch traced here: 291 us
  blocking collectives  169 us (57%)
  waiting for transfers between devices  38.7 us (13%)
  local copies, waits for them, and re-layouts  34.7 us (12%)
  matrix products  16.1 us (5%)
  other arithmetic  16 us (5%)
  between operations  15.9 us (5%)
    unnamed x1, blocking collectives  59 us
    pmax x1, blocking collectives, shards(): span_top, row_top = lax.pmax((span_peak, row_peak), 'tensor')  48.4 us
    unnamed x2, waiting for transfers between devices  38.7 us
    all_gather x1, blocking collectives, shards(): lax.all_gather(query_part, 'tensor', axis=1, tiled=True)  22.1 us
    all_gather x1, blocking collectives, shards(): shard_rows = lax.all_gather(normed, 'tensor', axis=0, tiled=True)  21.5 us
    all_gather x1, blocking collectives, shards(): lax.all_gather(keyval_part, 'tensor', axis=1, tiled=True)  18.1 us
    unnamed x120, local copies, waits for them, and re-layouts  12.8 us
  transfers between devices with their start and end apart: 1, of which 1 were waited for; matrix products, arithmetic and copies ran while one was open for 3% of the time, Pallas kernels for 0%

commit v1 on v0

v1 whole, which is shorter than its diff:
```python
import functools
import math

import jax
import jax.numpy as jnp
import numpy as np
from jax import lax
from jax.experimental import pallas as pl
from jax.experimental.pallas import tpu as pltpu
from jax.sharding import PartitionSpec as P

D = 8192
H = 64
KVH = 8
HD = 128
PAGE = 16
STEPS = 2
BLK_ROW = 32


epsilon = 1e-05
neg_fill = -1e30
rotation_bits = 20


def normalize(row_block, gain_vector):
    widened = row_block.astype(jnp.float32)
    mean_square = jnp.mean(widened * widened, axis=-1, keepdims=True)
    return (widened * lax.rsqrt(mean_square + epsilon) * gain_vector.astype(jnp.float32)).astype(
        jnp.bfloat16
    )


def llama_frequencies(half_width):
    exponents = np.arange(half_width) / (1.0 * half_width)
    inverse = 1.0 / 500000.0**exponents
    wavelen = 2.0 * np.pi / inverse
    scaled = np.where(wavelen > 8192.0, inverse / 8.0, inverse)
    smooth = (8192.0 / wavelen - 1.0) / 3.0
    blended = (1.0 - smooth) * inverse / 8.0 + smooth * inverse
    middle = (wavelen >= 2048.0) & (wavelen <= 8192.0)
    return np.where(middle, blended, scaled)


def rotation_tables(half_width):
    frequencies = llama_frequencies(half_width)
    powers = 2.0 ** np.arange(rotation_bits)
    angles = powers[:, None] * frequencies[None, :]
    return (jnp.asarray(np.cos(angles), jnp.float32), jnp.asarray(np.sin(angles), jnp.float32))


VMEM_BYTES = 60 * 1024 * 1024
VMEM_SPEC = pl.BlockSpec(memory_space=pltpu.VMEM)


def greet(count, me):
    barrier = pltpu.get_barrier_semaphore()

    def signal(i, carry):
        pl.semaphore_signal(
            barrier,
            inc=1,
            device_id={"tensor": lax.rem(me + i, count)},
            device_id_type=pl.DeviceIdType.MESH,
        )
        return carry

    lax.fori_loop(1, count, signal, 0)
    pl.semaphore_wait(barrier, count - 1)


def spread_kernel(count, arrays, *refs):
    sources, targets = refs[:arrays], refs[arrays : 2 * arrays]
    send_sems, recv_sems, local_sems = refs[2 * arrays :]
    me = lax.axis_index("tensor")
    locals_ = [
        pltpu.make_async_copy(sources[a], targets[a].at[me], local_sems.at[a])
        for a in range(arrays)
    ]
    for copy in locals_:
        copy.start()
    greet(count, me)

    def remote(a, i):
        return pltpu.make_async_remote_copy(
            src_ref=sources[a],
            dst_ref=targets[a].at[me],
            send_sem=send_sems.at[a, i],
            recv_sem=recv_sems.at[a, i],
            device_id={"tensor": lax.rem(me + i, count)},
            device_id_type=pl.DeviceIdType.MESH,
        )

    def start(i, carry):
        for a in range(arrays):
            remote(a, i).start()
        return carry

    def finish(i, carry):
        for a in range(arrays):
            remote(a, i).wait()
        return carry

    lax.fori_loop(1, count, start, 0)
    for copy in locals_:
        copy.wait()
    lax.fori_loop(1, count, finish, 0)


def spread(parts, count, collective_id):
    arrays = len(parts)
    return pl.pallas_call(
        functools.partial(spread_kernel, count, arrays),
        out_shape=[jax.ShapeDtypeStruct((count,) + p.shape, p.dtype) for p in parts],
        in_specs=[VMEM_SPEC] * arrays,
        out_specs=[VMEM_SPEC] * arrays,
        scratch_shapes=[
            pltpu.SemaphoreType.DMA((arrays, count)),
            pltpu.SemaphoreType.DMA((arrays, count)),
            pltpu.SemaphoreType.DMA((arrays,)),
        ],
        compiler_params=pltpu.CompilerParams(
            collective_id=collective_id, has_side_effects=True, vmem_limit_bytes=VMEM_BYTES
        ),
        name=f"spread_{collective_id}",
    )(*parts)


def attend_kernel(
    count,
    heads_at_once,
    q_ref,
    kv_ref,
    pk_ref,
    pv_ref,
    dk_ref,
    dv_ref,
    map_ref,
    pos_ref,
    cos_ref,
    sin_ref,
    part_ref,
    stat_ref,
    cache_ref,
    turn_cos,
    turn_sin,
    wide,
    stats,
):
    me = lax.axis_index("tensor")
    f32 = jnp.float32
    bf16 = jnp.bfloat16
    total = pos_ref.shape[0]
    group = H // KVH
    scale = 1.0 / math.sqrt(HD)
    positions = pos_ref[...]
    cos_part = jnp.ones((total, HD), f32)
    sin_part = jnp.zeros((total, HD), f32)
    for bit in range(rotation_bits):
        chosen = (positions >> bit & 1).astype(f32)
        step_cos = 1.0 + chosen * (cos_ref[bit : bit + 1, :] - 1.0)
        step_sin = chosen * sin_ref[bit : bit + 1, :]
        cos_part, sin_part = (
            cos_part * step_cos - sin_part * step_sin,
            sin_part * step_cos + cos_part * step_sin,
        )
    lanes = lax.broadcasted_iota(jnp.int32, (total, HD), 1)
    turn_cos[...] = cos_part
    turn_sin[...] = jnp.where(lanes < HD // 2, -sin_part, sin_part)

    def turn(x):
        wide_x = x.astype(f32)
        return (wide_x * turn_cos[...] + pltpu.roll(wide_x, HD // 2, 1) * turn_sin[...]).astype(bf16)

    prefix_dev = pk_ref.shape[0]
    slot = lax.broadcasted_iota(jnp.int32, (1, prefix_dev), 1)
    prefix_seen = me * prefix_dev + slot < positions[0:1, :]

    pool_dev = dk_ref.shape[0]
    block_dev = pool_dev // PAGE
    token = lax.broadcasted_iota(jnp.int32, (1, pool_dev), 1)
    block_of = me * block_dev + token // PAGE
    entries = map_ref.shape[0]
    entry = lax.broadcasted_iota(jnp.int32, (entries, 1), 0)
    found = jnp.sum(jnp.where(map_ref[...] == block_of, entry, 0), axis=0, keepdims=True)
    row_of = found // BLK_ROW
    place = (found % BLK_ROW) * PAGE + token % PAGE
    row_ids = lax.broadcasted_iota(jnp.int32, (count, 1), 0)
    lens = positions[count : 2 * count, :]
    length = jnp.sum(jnp.where(row_ids == row_of, lens, 0), axis=0, keepdims=True)
    key_row = jnp.where(place < length, row_of, -1)

    nh = heads_at_once
    span_q = lax.broadcasted_iota(jnp.int32, (nh * count, 1), 0) % count
    own_j = lax.broadcasted_iota(jnp.int32, (1, count), 1)
    span_own = (own_j == me) & (own_j <= span_q)
    dec_q = lax.broadcasted_iota(jnp.int32, (nh * STEPS * count, 1), 0)
    dec_row = dec_q % count
    dec_step = (dec_q // count) % STEPS
    new_j = lax.broadcasted_iota(jnp.int32, (1, STEPS * count), 1)
    dec_own = (new_j % count == me) & (dec_row == me) & (new_j // count <= dec_step)
    pick = lax.broadcasted_iota(jnp.int32, (count, 1), 0) == me
    stat_lane = lax.broadcasted_iota(jnp.int32, (count, 2 * H), 1)
    stats[...] = jnp.zeros_like(stats)
    stat_ref[...] = jnp.zeros_like(stat_ref)
    across = (((1,), (1,)), ((), ()))

    def soft(q, keys, values, seen, keys2, values2, seen2):
        s1 = lax.dot_general(q, keys, across, preferred_element_type=f32) * scale
        s2 = lax.dot_general(q, keys2, across, preferred_element_type=f32) * scale
        s1 = jnp.where(seen, s1, neg_fill)
        s2 = jnp.where(seen2, s2, neg_fill)
        top = jnp.maximum(
            jnp.max(s1, axis=1, keepdims=True), jnp.max(s2, axis=1, keepdims=True)
        )
        w1 = jnp.where(seen, jnp.exp(s1 - top), 0.0)
        w2 = jnp.where(seen2, jnp.exp(s2 - top), 0.0)
        den = jnp.sum(w1, axis=1, keepdims=True) + jnp.sum(w2, axis=1, keepdims=True)
        num = jnp.dot(w1.astype(bf16), values, preferred_element_type=f32) + jnp.dot(
            w2.astype(bf16), values2, preferred_element_type=f32
        )
        return top, den, num

    def per_head(g, carry):
        cols = pl.ds(pl.multiple_of(g * HD, HD), HD)
        new_keys = turn(kv_ref[g])
        new_values = kv_ref[KVH + g]
        cache_ref[pl.ds(g, 1), :] = jnp.sum(
            jnp.where(pick, new_keys[:count].astype(f32), 0.0), axis=0, keepdims=True
        )
        cache_ref[pl.ds(KVH + g, 1), :] = jnp.sum(
            jnp.where(pick, new_values[:count].astype(f32), 0.0), axis=0, keepdims=True
        )
        for first in range(0, group, nh):
            turned = [turn(q_ref[g * group + first + i]) for i in range(nh)]
            span_queries = jnp.concatenate([t[:count] for t in turned], axis=0)
            dec_queries = jnp.concatenate([t[count:] for t in turned], axis=0)
            span_top, span_den, span_num = soft(
                span_queries,
                pk_ref[:, cols],
                pv_ref[:, cols],
                prefix_seen,
                new_keys[:count],
                new_values[:count],
                span_own,
            )
            dec_top, dec_den, dec_num = soft(
                dec_queries,
                dk_ref[:, cols],
                dv_ref[:, cols],
                key_row == dec_row,
                new_keys[count:],
                new_values[count:],
                dec_own,
            )
            for i in range(nh):
                head = g * group + first + i
                for kind in range(1 + STEPS):
                    if kind == 0:
                        rows = slice(i * count, (i + 1) * count)
                        top, den, num = span_top[rows], span_den[rows], span_num[rows]
                    else:
                        at = (i * STEPS + kind - 1) * count
                        rows = slice(at, at + count)
                        top, den, num = dec_top[rows], dec_den[rows], dec_num[rows]
                    wide[kind, pl.ds(head, count, stride=H), :] = num
                    stats[kind] = jnp.where(
                        stat_lane == head,
                        top,
                        jnp.where(stat_lane == H + head, den, stats[kind]),
                    )
        return carry

    lax.fori_loop(0, KVH, per_head, 0)
    for kind in range(1 + STEPS):
        stat_ref[pl.ds(kind, count, stride=8), :] = stats[kind]

    def pack(d, carry):
        for kind in range(1 + STEPS):
            rows = pl.ds(pl.multiple_of(d * H, H), H)
            part_ref[d, kind * H : (kind + 1) * H, :] = wide[kind, rows, :].astype(bf16)
        return carry

    lax.fori_loop(0, count, pack, 0)


def merge_kernel(count, part_ref, stat_ref, out_ref, parts, stats, send_sems, recv_sems, local_sems):
    me = lax.axis_index("tensor")
    f32 = jnp.float32
    sources, targets = (part_ref, stat_ref), (parts, stats)
    locals_ = [
        pltpu.make_async_copy(sources[a].at[me], targets[a].at[me], local_sems.at[a])
        for a in range(2)
    ]
    for copy in locals_:
        copy.start()
    greet(count, me)

    def remote(a, i):
        peer = lax.rem(me + i, count)
        return pltpu.make_async_remote_copy(
            src_ref=sources[a].at[peer],
            dst_ref=targets[a].at[me],
            send_sem=send_sems.at[a, i],
            recv_sem=recv_sems.at[a, i],
            device_id={"tensor": peer},
            device_id_type=pl.DeviceIdType.MESH,
        )

    def start(i, carry):
        for a in range(2):
            remote(a, i).start()
        return carry

    def finish(i, carry):
        for a in range(2):
            remote(a, i).wait()
        return carry

    lax.fori_loop(1, count, start, 0)
    for copy in locals_:
        copy.wait()
    lax.fori_loop(1, count, finish, 0)
    top = stats[0]
    for d in range(1, count):
        top = jnp.maximum(top, stats[d])
    den = jnp.zeros_like(top)
    for d in range(count):
        den = den + jnp.exp(stats[d] - top) * pltpu.roll(stats[d], H, 1)
    inverse = 1.0 / den
    share = jnp.concatenate([jnp.exp(stats[d] - top) * inverse for d in range(count)], axis=0).T
    for kind in range(1 + STEPS):
        acc = jnp.zeros((H, HD), f32)
        for d in range(count):
            acc = acc + share[:H, d * 8 + kind : d * 8 + kind + 1] * parts[
                d, kind * H : (kind + 1) * H, :
            ].astype(f32)
        out_ref[kind] = acc.astype(out_ref.dtype)


def shards(
    span_rows,
    decode_rows,
    norm_gain,
    w_query,
    w_keyval,
    prefix_keys,
    prefix_values,
    span_offset,
    pool_keys,
    pool_values,
    row_blocks,
    context_lens,
):
    count = lax.axis_size("tensor")
    span_dev = span_rows.shape[0]
    rows_dev = decode_rows.shape[1]
    assert span_dev == 1 and rows_dev == 1
    kinds = 1 + STEPS
    local_rows = jnp.concatenate([span_rows, decode_rows.reshape(STEPS, D)], axis=0)
    normed = normalize(local_rows, norm_gain)
    (gathered,) = spread([normed.reshape(kinds * 16, D // 16)], count, 0)
    shard_rows = gathered.reshape(count, kinds, D).transpose(1, 0, 2).reshape(kinds * count, D)
    total = kinds * count
    queries = jnp.dot(shard_rows, w_query, preferred_element_type=jnp.float32).astype(jnp.bfloat16)
    keyval = jnp.dot(shard_rows, w_keyval, preferred_element_type=jnp.float32).astype(jnp.bfloat16)

    def split(x):
        if x.shape[1] % HD == 0:
            return x.reshape(total, -1, HD).transpose(1, 0, 2)
        return x

    def join(x):
        if x.ndim == 4:
            return x.reshape(-1, total, HD)
        return x.transpose(1, 0, 2).reshape(total, -1, HD).transpose(1, 0, 2)

    all_q, all_kv = spread([split(queries), split(keyval)], count, 1)
    q_heads, kv_heads = join(all_q), join(all_kv)
    offset = span_offset[0]
    positions = jnp.concatenate(
        [offset + jnp.arange(count, dtype=jnp.int32)] + [context_lens + s for s in range(STEPS)]
    )[:, None]
    cos_table, sin_table = rotation_tables(HD // 2)
    tile = lambda x: jnp.concatenate([x, x], axis=1)
    part, stat, cache = pl.pallas_call(
        functools.partial(attend_kernel, count, H // KVH if count <= 32 else 1),
        out_shape=[
            jax.ShapeDtypeStruct((count, kinds * H, HD), jnp.bfloat16),
            jax.ShapeDtypeStruct((count * 8, 2 * H), jnp.float32),
            jax.ShapeDtypeStruct((2 * KVH, HD), jnp.float32),
        ],
        in_specs=[VMEM_SPEC] * 10,
        out_specs=[VMEM_SPEC] * 3,
        scratch_shapes=[
            pltpu.VMEM((total, HD), jnp.float32),
            pltpu.VMEM((total, HD), jnp.float32),
            pltpu.VMEM((kinds, count * H, HD), jnp.float32),
            pltpu.VMEM((kinds, count, 2 * H), jnp.float32),
        ],
        compiler_params=pltpu.CompilerParams(vmem_limit_bytes=VMEM_BYTES),
        name="attend",
    )(
        q_heads,
        kv_heads,
        prefix_keys,
        prefix_values,
        pool_keys.reshape(-1, KVH * HD),
        pool_values.reshape(-1, KVH * HD),
        row_blocks.reshape(-1, 1),
        positions,
        tile(cos_table),
        tile(sin_table),
    )
    merged = pl.pallas_call(
        functools.partial(merge_kernel, count),
        out_shape=jax.ShapeDtypeStruct((kinds, H, HD), jnp.bfloat16),
        in_specs=[VMEM_SPEC] * 2,
        out_specs=VMEM_SPEC,
        scratch_shapes=[
            pltpu.VMEM((count, kinds * H, HD), jnp.bfloat16),
            pltpu.VMEM((count, 8, 2 * H), jnp.float32),
            pltpu.SemaphoreType.DMA((2, count)),
            pltpu.SemaphoreType.DMA((2, count)),
            pltpu.SemaphoreType.DMA((2,)),
        ],
        compiler_params=pltpu.CompilerParams(
            collective_id=2, has_side_effects=True, vmem_limit_bytes=VMEM_BYTES
        ),
        name="merge",
    )(part, stat.reshape(count, 8, 2 * H))
    span_attended = merged[0].reshape(1, D)
    decode_attended = merged[1:].reshape(STEPS, 1, D)
    span_cache = cache.reshape(1, 2 * KVH * HD).astype(jnp.bfloat16)
    return (span_attended, decode_attended, span_cache)


def solution(mesh):
    in_specs = (
        P(("groups", "tensor"), None),
        P(None, ("groups", "tensor"), None),
        P(),
        P(None, "tensor"),
        P(None, "tensor"),
        P(("groups", "tensor"), None),
        P(("groups", "tensor"), None),
        P("groups"),
        P(("groups", "tensor"), None, None),
        P(("groups", "tensor"), None, None),
        P("groups", None),
        P("groups"),
    )
    out_specs = (
        P(("groups", "tensor"), None),
        P(None, ("groups", "tensor"), None),
        P(("groups", "tensor"), None),
    )
    return jax.shard_map(shards, mesh=mesh, in_specs=in_specs, out_specs=out_specs, check_vma=False)
```

time: 295 us -> 114 us (0.39); the launches traced: 291 us -> 113 us
  blocking collectives: 169 us -> 0 us
  Pallas kernels: 0 us -> 90 us
  waiting for transfers between devices: 38.7 us -> 0 us
  local copies, waits for them, and re-layouts: 34.7 us -> 10.6 us
  between operations: 15.9 us -> 1.51 us
  other arithmetic: 16 us -> 4.62 us
  matrix products: 16.1 us -> 6 us
    pallas_call x0 -> x4, Pallas kernels: none -> 90 us  [the longest x2 51.9 us: spread(): pl.pallas_call(functools.partial(spread_kernel, count, arrays), out_shape...]
    all_gather x3 -> x0, blocking collectives: 61.7 us -> none  [the longest x1 22.1 us: shards(): lax.all_gather(query_part, 'tensor', axis=1, tiled=True)]
    unnamed x1 -> x0, blocking collectives: 59 us -> none
    pmax x1 -> x0, blocking collectives: 48.4 us -> none  [shards(): span_top, row_top = lax.pmax((span_peak, row_peak), 'tensor')]
    unnamed x2 -> x0, waiting for transfers between devices: 38.7 us -> none
    unnamed x120 -> x5, local copies, waits for them, and re-layouts: 12.8 us -> 1.97 us
    dot_general x10 -> x2, matrix products: 16.1 us -> 6 us  [the longest x1 4.91 us: shards(): jnp.dot(shard_rows, w_query, preferred_element_type=jnp.float32)]
    gather x6 -> x0, local copies, waits for them, and re-layouts: 7.3 us -> none  [the longest x2 5.17 us: shards(): jnp.take(decode_queries, block_rows, axis=0)]
  transfers between devices with their start and end apart: 1 -> 0, of which waited for: 1 -> 0; matrix products, arithmetic and copies ran while one was open for 3% -> 0% of each run, Pallas kernels for 0% -> 0%
where the time goes in v1:
time: 114 us; the launch traced here: 113 us
  Pallas kernels  90 us (79%)
  local copies, waits for them, and re-layouts  10.6 us (9%)
  matrix products  6 us (5%)
  other arithmetic  4.62 us (4%)
  between operations  1.51 us (1%)
    pallas_call x2, Pallas kernels, spread(): pl.pallas_call(functools.partial(spread_kernel, count, arrays), out_shape...  51.9 us
    pallas_call x1, Pallas kernels, shards(): pl.pallas_call(functools.partial(merge_kernel, count), out_shape=jax.Shap...  25.7 us
    pallas_call x1, Pallas kernels, shards(): pl.pallas_call(functools.partial(attend_kernel, count, H // KVH if count...  12.4 us
    dot_general x1, matrix products, shards(): jnp.dot(shard_rows, w_query, preferred_element_type=jnp.float32)  4.91 us
    reshape x1, local copies, waits for them, and re-layouts, shards(): gathered.reshape(count, kinds, D).transpose(1, 0, 2)  2.74 us

profile of v1, /device:TPU:13, one launch (start us, length us, event | category | flops | bytes accessed | tf_op | source)
XLA Modules:
  0.0 112.8 jit_solution(4117881410201141536)
XLA Ops:
  0.6 0.0 copy-start
  1.4 1.0 multiply_reduce_fusion
  2.4 0.7 iota_add_fusion
  3.1 0.7 add_bitcast_fusion
  3.8 0.1 mul.32
  3.9 0.1 mul.33
  4.0 0.7 copy.21.pos_ref
  4.7 0.7 reshape.83
  5.4 0.8 maximum_convert_fusion
  6.3 0.1 reshape.82
  6.3 0.7 fusion.2.refs_0_
  7.0 1.7 %reshape.84.map_ref = s32[512,1]{1,0:T(8,128)} reshape(s32[16,32]{1,0:T(8,128)} %param.24) | data formatting | bytes 4096 | tf_op jit(solution)/shard_map/reshape | solution.py:410
  8.7 24.1 %spread_0.1 = bf16[16,48,512]{2,1,0:T(8,128)(2,1)} custom-call(bf16[48,512]{1,0:T(8,128)(2,1)} %fusion.2.refs_0_), custom_call_target="tpu_custom_call" | custom-call | tf_op jit(solution)/shard_map/spread_0/pallas_call | solution.py:112
  32.8 2.7 %reshape.72 = bf16[16,3,8192]{2,1,0:T(4,128)(2,1)S(1)} reshape(bf16[16,48,512]{2,1,0:T(8,128)(2,1)} %spread_0.1) | data formatting | bytes 1572864 | tf_op jit(solution)/shard_map/reshape | solution.py:363
  35.5 0.6 copy.18
  36.1 0.0 copy-done
  36.1 1.1 fusion.1.refs_1_
  37.2 4.9 %fusion = bf16[6,4,8,128]{3,2,1,0:T(8,128)(2,1)S(1)} fusion(bf16[48,8192]{1,0:T(8,128)(2,1)S(1)} %bitcast.42, bf16[8192,512]{1,0:T(8,128)(2,1)} %param.17), kind=kOutput, calls=%fused_computation.1 | convolution fusion | flops 402677760 | bytes 9224192 | tf_op jit(solution)/shard_map/dot_general | solution.py:365
  42.1 0.6 copy.28
  42.8 27.8 %spread_1.1 = (bf16[16,4,48,128]{3,2,1,0:T(8,128)(2,1)}, bf16[16,1,48,128]{3,2,1,0:T(8,128)(2,1)}) custom-call(bf16[4,48,128]{2,1,0:T(8,128)(2,1)} %bitcast.48, bf16[1,48,128]{2,1,0:T(8,128)(2,1)} %fusion.1.refs_1_), custom_call_target="tpu_custom_call" | custom-call | tf_op jit(solution)/shard_map/spread_1/pallas_call | solution.py:112
  70.6 12.4 %attend.1 = (bf16[16,192,128]{2,1,0:T(8,128)(2,1)}, f32[128,128]{1,0:T(8,128)}, f32[16,128]{1,0:T(8,128)}) custom-call(bf16[64,48,128]{2,1,0:T(8,128)(2,1)} %bitcast.46, bf16[16,48,128]{2,1,0:T(8,128)(2,1)} %bitcast.47, bf16[256,1024]{1,0:T(8,128)(2,1)} %pk_ref.1, bf16[256,1024]{1,0:T(8,128)(2,1)} %pv_ref.1, bf16[512,1024]{1,0:T(8,128)(2,1)} %bitcast.44, ...), custom_call_target="tpu_custom_call" | custom-call | tf_op jit(solution)/shard_map/attend/pallas_call | solution.py:386
  83.0 25.7 %merge.1 = bf16[3,64,128]{2,1,0:T(8,128)(2,1)} custom-call(bf16[16,192,128]{2,1,0:T(8,128)(2,1)} %get-tuple-element.10.part_ref, f32[16,8,128]{2,1,0:T(8,128)} %bitcast.51), custom_call_target="tpu_custom_call" | custom-call | tf_op jit(solution)/shard_map/merge/pallas_call | solution.py:415
  108.7 0.7 convert_bitcast_fusion
  109.4 0.6 copy.30
  110.0 0.7 slice_bitcast_fusion
  110.7 0.8 slice.7
  111.5 0.6 reshape.81
  112.1 0.6 copy.29
  (1 shorter events, 0.0 us)
Async XLA Ops:
  0.6 35.5 %copy-start = (bf16[8192,128]{1,0:T(8,128)(2,1)S(1)}, bf16[8192,128]{1,0:T(8,128)(2,1)}, u32[]{:S(2)}) copy-start(bf16[8192,128]{1,0:T(8,128)(2,1)} %param.18) | copy-start | bytes 6291460

commit v2 on v1

--- a/solution.py
+++ b/solution.py
@@ -69,68 +69,123 @@
     pl.semaphore_wait(barrier, count - 1)
 
 
-def spread_kernel(count, arrays, *refs):
-    sources, targets = refs[:arrays], refs[arrays : 2 * arrays]
-    send_sems, recv_sems, local_sems = refs[2 * arrays :]
+def layout_of(mesh):
+    count = mesh.shape["tensor"]
+    line = mesh.devices.reshape(-1, count)[0]
+    coords = [tuple(getattr(device, "coords", (i,))) for i, device in enumerate(line)]
+    cores = sum(1 for c in coords if c == coords[0])
+    chips = coords[::cores]
+    inner = 1
+    if len(chips) > 1:
+        axis = [p != q for p, q in zip(chips[0], chips[1])].index(True)
+        inner = len({c[axis] for c in chips})
+    if count % (cores * inner):
+        return count, 1, 1
+    return count // (cores * inner), inner, cores
+
+
+def spread_copies(layout, source, target, send_sems, recv_sems):
+    outer, inner, cores = layout
     me = lax.axis_index("tensor")
-    locals_ = [
-        pltpu.make_async_copy(sources[a], targets[a].at[me], local_sems.at[a])
-        for a in range(arrays)
-    ]
-    for copy in locals_:
+    core = lax.rem(me, cores)
+    column = lax.rem(me // cores, inner)
+    plane = me // (cores * inner)
+    pending = []
+
+    def index(z, y, c):
+        return (z * inner + y) * cores + c
+
+    def send(owner, src, peer, slot):
+        copy = pltpu.make_async_remote_copy(
+            src_ref=src,
+            dst_ref=target.at[owner],
+            send_sem=send_sems.at[slot],
+            recv_sem=recv_sems.at[owner],
+            device_id={"tensor": peer},
+            device_id_type=pl.DeviceIdType.MESH,
+        )
         copy.start()
+        pending.append(copy)
+
+    def arrived(owner):
+        pltpu.make_async_remote_copy(
+            src_ref=source,
+            dst_ref=target.at[owner],
+            send_sem=send_sems.at[0],
+            recv_sem=recv_sems.at[owner],
+            device_id={"tensor": index(plane, column, lax.rem(core + 1, cores))},
+            device_id_type=pl.DeviceIdType.MESH,
+        ).wait_recv()
+
+    slots = iter(range(outer * inner * cores))
+    for i in range(1, outer):
+        send(me, source, index(lax.rem(plane + i, outer), column, core), next(slots))
+    for j in range(outer):
+        owner = index(lax.rem(plane + outer - j, outer), column, core)
+        if j > 0:
+            arrived(owner)
+        src = source if j == 0 else target.at[owner]
+        for k in range(1, inner):
+            send(owner, src, index(plane, lax.rem(column + k, inner), core), next(slots))
+        for k in range(1, cores):
+            send(owner, src, index(plane, column, lax.rem(core + k, cores)), next(slots))
+    for j in range(outer):
+        for k in range(1, inner):
+            owner = index(
+                lax.rem(plane + outer - j, outer), lax.rem(column + inner - k, inner), core
+            )
+            arrived(owner)
+            for n in range(1, cores):
+                peer = index(plane, column, lax.rem(core + n, cores))
+                send(owner, target.at[owner], peer, next(slots))
+    for j in range(outer):
+        for k in range(inner):
+            for n in range(1, cores):
+                arrived(
+                    index(
+                        lax.rem(plane + outer - j, outer),
+                        lax.rem(column + inner - k, inner),
+                        lax.rem(core + cores - n, cores),
+                    )
+                )
+    for copy in pending:
+        copy.wait_send()
+
+
+def spread_kernel(layout, source, target, send_sems, recv_sems, local_sem):
+    count = math.prod(layout)
+    me = lax.axis_index("tensor")
+    own = pltpu.make_async_copy(source, target.at[me], local_sem)
+    own.start()
     greet(count, me)
-
-    def remote(a, i):
-        return pltpu.make_async_remote_copy(
-            src_ref=sources[a],
-            dst_ref=targets[a].at[me],
-            send_sem=send_sems.at[a, i],
-            recv_sem=recv_sems.at[a, i],
-            device_id={"tensor": lax.rem(me + i, count)},
-            device_id_type=pl.DeviceIdType.MESH,
-        )
-
-    def start(i, carry):
-        for a in range(arrays):
-            remote(a, i).start()
-        return carry
-
-    def finish(i, carry):
-        for a in range(arrays):
-            remote(a, i).wait()
-        return carry
-
-    lax.fori_loop(1, count, start, 0)
-    for copy in locals_:
-        copy.wait()
-    lax.fori_loop(1, count, finish, 0)
-
-
-def spread(parts, count, collective_id):
-    arrays = len(parts)
+    spread_copies(layout, source, target, send_sems, recv_sems)
+    own.wait()
+
+
+def spread(part, layout, collective_id):
+    count = math.prod(layout)
     return pl.pallas_call(
-        functools.partial(spread_kernel, count, arrays),
-        out_shape=[jax.ShapeDtypeStruct((count,) + p.shape, p.dtype) for p in parts],
-        in_specs=[VMEM_SPEC] * arrays,
-        out_specs=[VMEM_SPEC] * arrays,
+        functools.partial(spread_kernel, layout),
+        out_shape=jax.ShapeDtypeStruct((count,) + part.shape, part.dtype),
+        in_specs=[VMEM_SPEC],
+        out_specs=VMEM_SPEC,
         scratch_shapes=[
-            pltpu.SemaphoreType.DMA((arrays, count)),
-            pltpu.SemaphoreType.DMA((arrays, count)),
-            pltpu.SemaphoreType.DMA((arrays,)),
+            pltpu.SemaphoreType.DMA((count,)),
+            pltpu.SemaphoreType.DMA((count,)),
+            pltpu.SemaphoreType.DMA,
         ],
         compiler_params=pltpu.CompilerParams(
             collective_id=collective_id, has_side_effects=True, vmem_limit_bytes=VMEM_BYTES
         ),
         name=f"spread_{collective_id}",
-    )(*parts)
+    )(part)
 
 
 def attend_kernel(
     count,
     heads_at_once,
-    q_ref,
-    kv_ref,
+    per_dev,
+    all_ref,
     pk_ref,
     pv_ref,
     dk_ref,
@@ -152,6 +207,14 @@
     bf16 = jnp.bfloat16
     total = pos_ref.shape[0]
     group = H // KVH
+    q_dev, kv_dev = per_dev
+
+    def q_head(h):
+        return all_ref[h // q_dev, h % q_dev]
+
+    def kv_head(j):
+        return all_ref[j // kv_dev, q_dev + j % kv_dev]
+
     scale = 1.0 / math.sqrt(HD)
     positions = pos_ref[...]
     cos_part = jnp.ones((total, HD), f32)
@@ -223,8 +286,8 @@
 
     def per_head(g, carry):
         cols = pl.ds(pl.multiple_of(g * HD, HD), HD)
-        new_keys = turn(kv_ref[g])
-        new_values = kv_ref[KVH + g]
+        new_keys = turn(kv_head(g))
+        new_values = kv_head(KVH + g)
         cache_ref[pl.ds(g, 1), :] = jnp.sum(
             jnp.where(pick, new_keys[:count].astype(f32), 0.0), axis=0, keepdims=True
         )
@@ -232,7 +295,7 @@
             jnp.where(pick, new_values[:count].astype(f32), 0.0), axis=0, keepdims=True
         )
         for first in range(0, group, nh):
-            turned = [turn(q_ref[g * group + first + i]) for i in range(nh)]
+            turned = [turn(q_head(g * group + first + i)) for i in range(nh)]
             span_queries = jnp.concatenate([t[:count] for t in turned], axis=0)
             dec_queries = jnp.concatenate([t[count:] for t in turned], axis=0)
             span_top, span_den, span_num = soft(
@@ -339,6 +402,7 @@
 
 
 def shards(
+    layout,
     span_rows,
     decode_rows,
     norm_gain,
@@ -359,24 +423,24 @@
     kinds = 1 + STEPS
     local_rows = jnp.concatenate([span_rows, decode_rows.reshape(STEPS, D)], axis=0)
     normed = normalize(local_rows, norm_gain)
-    (gathered,) = spread([normed.reshape(kinds * 16, D // 16)], count, 0)
+    gathered = spread(normed.reshape(kinds * 16, D // 16), layout, 0)
     shard_rows = gathered.reshape(count, kinds, D).transpose(1, 0, 2).reshape(kinds * count, D)
     total = kinds * count
     queries = jnp.dot(shard_rows, w_query, preferred_element_type=jnp.float32).astype(jnp.bfloat16)
     keyval = jnp.dot(shard_rows, w_keyval, preferred_element_type=jnp.float32).astype(jnp.bfloat16)
 
-    def split(x):
-        if x.shape[1] % HD == 0:
-            return x.reshape(total, -1, HD).transpose(1, 0, 2)
-        return x
-
-    def join(x):
-        if x.ndim == 4:
-            return x.reshape(-1, total, HD)
-        return x.transpose(1, 0, 2).reshape(total, -1, HD).transpose(1, 0, 2)
-
-    all_q, all_kv = spread([split(queries), split(keyval)], count, 1)
-    q_heads, kv_heads = join(all_q), join(all_kv)
+    q_dev, kv_dev = queries.shape[1] // HD, keyval.shape[1] // HD
+    if queries.shape[1] % HD == 0 and keyval.shape[1] % HD == 0:
+        heads = jnp.concatenate([queries, keyval], axis=1).reshape(total, -1, HD)
+        heads = spread(heads.transpose(1, 0, 2), layout, 1)
+    else:
+        cut = queries.shape[1]
+        heads = spread(jnp.concatenate([queries, keyval], axis=1), layout, 1).transpose(1, 0, 2)
+        heads = jnp.concatenate(
+            [heads[:, :, :cut].reshape(total, -1, HD), heads[:, :, cut:].reshape(total, -1, HD)],
+            axis=1,
+        ).transpose(1, 0, 2)[None]
+        q_dev, kv_dev = H, 2 * KVH
     offset = span_offset[0]
     positions = jnp.concatenate(
         [offset + jnp.arange(count, dtype=jnp.int32)] + [context_lens + s for s in range(STEPS)]
@@ -384,13 +448,15 @@
     cos_table, sin_table = rotation_tables(HD // 2)
     tile = lambda x: jnp.concatenate([x, x], axis=1)
     part, stat, cache = pl.pallas_call(
-        functools.partial(attend_kernel, count, H // KVH if count <= 32 else 1),
+        functools.partial(
+            attend_kernel, count, H // KVH if count <= 32 else 1, (q_dev, kv_dev)
+        ),
         out_shape=[
             jax.ShapeDtypeStruct((count, kinds * H, HD), jnp.bfloat16),
             jax.ShapeDtypeStruct((count * 8, 2 * H), jnp.float32),
             jax.ShapeDtypeStruct((2 * KVH, HD), jnp.float32),
         ],
-        in_specs=[VMEM_SPEC] * 10,
+        in_specs=[VMEM_SPEC] * 9,
         out_specs=[VMEM_SPEC] * 3,
         scratch_shapes=[
             pltpu.VMEM((total, HD), jnp.float32),
@@ -401,8 +467,7 @@
         compiler_params=pltpu.CompilerParams(vmem_limit_bytes=VMEM_BYTES),
         name="attend",
     )(
-        q_heads,
-        kv_heads,
+        heads,
         prefix_keys,
         prefix_values,
         pool_keys.reshape(-1, KVH * HD),
@@ -455,4 +520,10 @@
         P(None, ("groups", "tensor"), None),
         P(("groups", "tensor"), None),
     )
-    return jax.shard_map(shards, mesh=mesh, in_specs=in_specs, out_specs=out_specs, check_vma=False)
+    return jax.shard_map(
+        functools.partial(shards, layout_of(mesh)),
+        mesh=mesh,
+        in_specs=in_specs,
+        out_specs=out_specs,
+        check_vma=False,
+    )

time: 114 us -> 93.9 us (0.82)
  Pallas kernels: 90 us -> 71 us
    pallas_call x2, Pallas kernels: 51.9 us -> 32 us  [spread(): pl.pallas_call(functools.partial(spread_kernel, layout), out_shape=jax.Sh...]
where the time goes in v2:
time: 93.9 us; the launch traced here: 93.2 us
  Pallas kernels  71 us (76%)
  local copies, waits for them, and re-layouts  10 us (11%)
  matrix products  5.4 us (6%)
  other arithmetic  5.26 us (6%)
  between operations  1.52 us (2%)
    pallas_call x2, Pallas kernels, spread(): pl.pallas_call(functools.partial(spread_kernel, layout), out_shape=jax.Sh...  32 us
    pallas_call x1, Pallas kernels, shards(): pl.pallas_call(functools.partial(merge_kernel, count), out_shape=jax.Shap...  26.4 us
    pallas_call x1, Pallas kernels, shards(): pl.pallas_call(functools.partial(attend_kernel, count, H // KVH if count...  12.6 us
    dot_general x1, matrix products, shards(): jnp.dot(shard_rows, w_query, preferred_element_type=jnp.float32)  4.91 us
    reshape x1, local copies, waits for them, and re-layouts, shards(): gathered.reshape(count, kinds, D).transpose(1, 0, 2)  2.74 us
    unnamed x5, local copies, waits for them, and re-layouts  1.97 us

profile of v2, /device:TPU:13, one launch (start us, length us, event | category | flops | bytes accessed | tf_op | source)
XLA Modules:
  0.0 93.2 jit_solution(16364617500318971081)
XLA Ops:
  0.6 0.0 copy-start
  1.4 1.0 %multiply_reduce_fusion = f32[3]{0:T(128)S(1)} fusion(bf16[2,8192]{1,0:T(2,128)(2,1)} %bitcast.41, bf16[1,8192]{1,0:T(2,128)(2,1)} %param.14), kind=kLoop, calls=%fused_computation.2 | loop fusion | flops 147453 | bytes 49164 | tf_op jit(solution)/shard_map/reduce_sum | solution.py:28
  2.4 0.7 iota_add_fusion
  3.1 0.7 add_bitcast_fusion
  3.8 0.1 mul.32
  3.9 0.1 mul.33
  4.0 0.7 copy.21.pos_ref
  4.7 0.7 reshape.75
  5.4 0.8 maximum_convert_fusion
  6.3 0.1 reshape.74
  6.3 0.7 fusion.source
  7.0 1.7 %reshape.76.map_ref = s32[512,1]{1,0:T(8,128)} reshape(s32[16,32]{1,0:T(8,128)} %param.24) | data formatting | bytes 4096 | tf_op jit(solution)/shard_map/reshape | solution.py:475
  8.7 15.5 %spread_0.1 = bf16[16,48,512]{2,1,0:T(8,128)(2,1)} custom-call(bf16[48,512]{1,0:T(8,128)(2,1)} %fusion.source), custom_call_target="tpu_custom_call" | custom-call | tf_op jit(solution)/shard_map/spread_0/pallas_call | solution.py:167
  24.2 2.7 %reshape.66 = bf16[16,3,8192]{2,1,0:T(4,128)(2,1)S(1)} reshape(bf16[16,48,512]{2,1,0:T(8,128)(2,1)} %spread_0.1) | data formatting | bytes 1572864 | tf_op jit(solution)/shard_map/reshape | solution.py:427
  26.9 0.6 copy.18
  27.5 0.0 copy-done
  27.5 0.5 convolution_convert_fusion.1
  28.0 4.9 %convolution_convert_fusion = bf16[48,512]{1,0:T(8,128)(2,1)S(1)} fusion(bf16[48,8192]{1,0:T(8,128)(2,1)S(1)} %bitcast.37, bf16[8192,512]{1,0:T(8,128)(2,1)} %param.17), kind=kOutput, calls=%fused_computation | convolution fusion | flops 402677760 | bytes 9224192 | tf_op jit(solution)/shard_map/dot_general | solution.py:429
  32.9 0.6 bitcast_bitcast_fusion.source
  33.6 16.5 %spread_1.1.all_ref = bf16[16,5,48,128]{3,2,1,0:T(8,128)(2,1)} custom-call(bf16[5,48,128]{2,1,0:T(8,128)(2,1)} %bitcast_bitcast_fusion.source), custom_call_target="tpu_custom_call" | custom-call | tf_op jit(solution)/shard_map/spread_1/pallas_call | solution.py:167
  50.1 12.6 %attend.1 = (bf16[16,192,128]{2,1,0:T(8,128)(2,1)}, f32[128,128]{1,0:T(8,128)}, f32[16,128]{1,0:T(8,128)}) custom-call(bf16[16,5,48,128]{3,2,1,0:T(8,128)(2,1)} %spread_1.1.all_ref, bf16[256,1024]{1,0:T(8,128)(2,1)} %pk_ref.1, bf16[256,1024]{1,0:T(8,128)(2,1)} %pv_ref.1, bf16[512,1024]{1,0:T(8,128)(2,1)} %bitcast.39, bf16[512,1024]{1,0:T(8,128)(2,1)} %bitcast.40, ...), custom_call_target="tpu_custom_call" | custom-call | tf_op jit(solution)/shard_map/attend/pallas_call | solution.py:450
  62.7 26.4 %merge.1 = bf16[3,64,128]{2,1,0:T(8,128)(2,1)} custom-call(bf16[16,192,128]{2,1,0:T(8,128)(2,1)} %get-tuple-element.6.part_ref, f32[16,8,128]{2,1,0:T(8,128)} %bitcast.43), custom_call_target="tpu_custom_call" | custom-call | tf_op jit(solution)/shard_map/merge/pallas_call | solution.py:480
  89.1 0.7 convert_bitcast_fusion
  89.8 0.6 copy.29
  90.4 0.7 slice_bitcast_fusion
  91.2 0.8 slice.7
  91.9 0.6 reshape.73
  92.6 0.6 copy.28
  (1 shorter events, 0.0 us)
Async XLA Ops:
  0.6 26.9 %copy-start = (bf16[8192,128]{1,0:T(8,128)(2,1)S(1)}, bf16[8192,128]{1,0:T(8,128)(2,1)}, u32[]{:S(2)}) copy-start(bf16[8192,128]{1,0:T(8,128)(2,1)} %param.18) | copy-start | bytes 6291460

commit v3 on v2

--- a/solution.py
+++ b/solution.py
@@ -20,15 +20,8 @@
 
 epsilon = 1e-05
 neg_fill = -1e30
+top_floor = -1e20
 rotation_bits = 20
-
-
-def normalize(row_block, gain_vector):
-    widened = row_block.astype(jnp.float32)
-    mean_square = jnp.mean(widened * widened, axis=-1, keepdims=True)
-    return (widened * lax.rsqrt(mean_square + epsilon) * gain_vector.astype(jnp.float32)).astype(
-        jnp.bfloat16
-    )
 
 
 def llama_frequencies(half_width):
@@ -53,7 +46,7 @@
 VMEM_SPEC = pl.BlockSpec(memory_space=pltpu.VMEM)
 
 
-def greet(count, me):
+def greet_all(count, me):
     barrier = pltpu.get_barrier_semaphore()
 
     def signal(i, carry):
@@ -67,6 +60,26 @@
 
     lax.fori_loop(1, count, signal, 0)
     pl.semaphore_wait(barrier, count - 1)
+
+
+def greet_near(layout):
+    outer, inner, cores = layout
+    me = lax.axis_index("tensor")
+    core = lax.rem(me, cores)
+    column = lax.rem(me // cores, inner)
+    plane = me // (cores * inner)
+    peers = [(lax.rem(plane + i, outer) * inner + column) * cores + core for i in range(1, outer)]
+    peers += [(plane * inner + lax.rem(column + i, inner)) * cores + core for i in range(1, inner)]
+    peers += [(plane * inner + column) * cores + lax.rem(core + i, cores) for i in range(1, cores)]
+    barrier = pltpu.get_barrier_semaphore()
+    for peer in peers:
+        pl.semaphore_signal(
+            barrier,
+            inc=1,
+            device_id={"tensor": peer},
+            device_id_type=pl.DeviceIdType.MESH,
+        )
+    pl.semaphore_wait(barrier, len(peers))
 
 
 def layout_of(mesh):
@@ -84,13 +97,14 @@
     return count // (cores * inner), inner, cores
 
 
-def spread_copies(layout, source, target, send_sems, recv_sems):
+def spread_copies(layout, target, send_sems, recv_sems):
     outer, inner, cores = layout
     me = lax.axis_index("tensor")
     core = lax.rem(me, cores)
     column = lax.rem(me // cores, inner)
     plane = me // (cores * inner)
     pending = []
+    source = target.at[me]
 
     def index(z, y, c):
         return (z * inner + y) * cores + c
@@ -152,33 +166,128 @@
         copy.wait_send()
 
 
-def spread_kernel(layout, source, target, send_sems, recv_sems, local_sem):
+def front_kernel(
+    layout,
+    span_ref,
+    decode_ref,
+    gain_ref,
+    wq_hbm,
+    wkv_hbm,
+    heads_ref,
+    lines,
+    gathered,
+    spread_rows,
+    wq_buf,
+    wkv_buf,
+    weight_sems,
+    send_sems,
+    recv_sems,
+    send_sems2,
+    recv_sems2,
+):
+    f32 = jnp.float32
     count = math.prod(layout)
     me = lax.axis_index("tensor")
-    own = pltpu.make_async_copy(source, target.at[me], local_sem)
-    own.start()
-    greet(count, me)
-    spread_copies(layout, source, target, send_sems, recv_sems)
-    own.wait()
-
-
-def spread(part, layout, collective_id):
+    depth, pieces = wq_hbm.shape[0], weight_sems.shape[1]
+    step = depth // pieces
+    fetches = []
+    for i in range(pieces):
+        rows = pl.ds(i * step, step)
+        for a, (src, dst) in enumerate(((wq_hbm, wq_buf), (wkv_hbm, wkv_buf))):
+            copy = pltpu.make_async_copy(src.at[rows], dst.at[rows], weight_sems.at[a, i])
+            copy.start()
+            fetches.append(copy)
+    gain = gain_ref[...].astype(f32)
+    width = lines.shape[1]
+    folds = depth // width
+    kinds = lines.shape[0] // folds
+    for first, ref in ((0, span_ref), (1, decode_ref)):
+        x = ref[...].astype(f32)
+        mean_square = jnp.mean(x * x, axis=-1, keepdims=True)
+        x = x * lax.rsqrt(mean_square + epsilon) * gain
+        for r in range(x.shape[0]):
+            for k in range(folds):
+                lines[pl.ds((first + r) * folds + k, 1), :] = x[
+                    r : r + 1, k * width : (k + 1) * width
+                ]
+    gathered[me] = lines[...].astype(jnp.bfloat16)
+    greet_near(layout)
+    spread_copies(layout, gathered, send_sems, recv_sems)
+
+    def widen(d, carry):
+        rows = pl.ds(pl.multiple_of(d * kinds * folds, kinds * folds), kinds * folds)
+        for j in range(width // HD):
+            spread_rows[j, rows, :] = gathered[d, :, j * HD : (j + 1) * HD].astype(f32)
+        return carry
+
+    lax.fori_loop(0, count, widen, 0)
+    total = kinds * count
+    queries = jnp.zeros((total, wq_hbm.shape[1]), f32)
+    keyval = jnp.zeros((total, wkv_hbm.shape[1]), f32)
+    for k in range(folds):
+        if k * width % step == 0:
+            at = k * width // step
+            fetches[2 * at].wait()
+            fetches[2 * at + 1].wait()
+        rows = jnp.concatenate(
+            [
+                jnp.concatenate(
+                    [
+                        spread_rows[j, pl.ds(kind * folds + k, count, stride=kinds * folds), :]
+                        for kind in range(kinds)
+                    ],
+                    axis=0,
+                )
+                for j in range(width // HD)
+            ],
+            axis=1,
+        ).astype(jnp.bfloat16)
+        part = slice(k * width, (k + 1) * width)
+        queries += jnp.dot(rows, wq_buf[part, :], preferred_element_type=f32)
+        keyval += jnp.dot(rows, wkv_buf[part, :], preferred_element_type=f32)
+    if len(heads_ref.shape) == 4:
+        q_dev = queries.shape[1] // HD
+        for h in range(heads_ref.shape[1]):
+            x = queries if h < q_dev else keyval
+            at = (h if h < q_dev else h - q_dev) * HD
+            heads_ref[me, h] = x[:, at : at + HD].astype(jnp.bfloat16)
+    else:
+        heads_ref[me] = jnp.concatenate([queries, keyval], axis=1).astype(jnp.bfloat16)
+    spread_copies(layout, heads_ref, send_sems2, recv_sems2)
+
+
+def front(layout, span_rows, decode_rows, norm_gain, w_query, w_keyval):
     count = math.prod(layout)
+    kinds = 1 + STEPS
+    total = kinds * count
+    depth, q_cols = w_query.shape
+    kv_cols = w_keyval.shape[1]
+    width = 512
+    by_head = q_cols % HD == 0 and kv_cols % HD == 0
+    heads = ((q_cols + kv_cols) // HD, total, HD) if by_head else (total, q_cols + kv_cols)
+    dma = pltpu.SemaphoreType.DMA
     return pl.pallas_call(
-        functools.partial(spread_kernel, layout),
-        out_shape=jax.ShapeDtypeStruct((count,) + part.shape, part.dtype),
-        in_specs=[VMEM_SPEC],
+        functools.partial(front_kernel, layout),
+        out_shape=jax.ShapeDtypeStruct((count,) + heads, jnp.bfloat16),
+        in_specs=[VMEM_SPEC] * 3 + [pl.BlockSpec(memory_space=pl.ANY)] * 2,
         out_specs=VMEM_SPEC,
         scratch_shapes=[
-            pltpu.SemaphoreType.DMA((count,)),
-            pltpu.SemaphoreType.DMA((count,)),
-            pltpu.SemaphoreType.DMA,
+            pltpu.VMEM((kinds * depth // width, width), jnp.float32),
+            pltpu.VMEM((count, kinds * depth // width, width), jnp.bfloat16),
+            pltpu.VMEM((width // HD, count * kinds * depth // width, HD), jnp.float32),
+            pltpu.VMEM(w_query.shape, jnp.bfloat16),
+            pltpu.VMEM(w_keyval.shape, jnp.bfloat16),
+            dma((2, 4)),
+            dma((count,)),
+            dma((count,)),
+            dma((count,)),
+            dma((count,)),
         ],
         compiler_params=pltpu.CompilerParams(
-            collective_id=collective_id, has_side_effects=True, vmem_limit_bytes=VMEM_BYTES
+            collective_id=0, has_side_effects=True, vmem_limit_bytes=VMEM_BYTES
         ),
-        name=f"spread_{collective_id}",
-    )(part)
+        name="front",
+    )(span_rows, decode_rows.reshape(STEPS, depth), norm_gain.reshape(1, depth), w_query, w_keyval)
 
 
 def attend_kernel(
@@ -191,7 +300,8 @@
     dk_ref,
     dv_ref,
     map_ref,
-    pos_ref,
+    offset_ref,
+    lens_ref,
     cos_ref,
     sin_ref,
     part_ref,
@@ -205,7 +315,7 @@
     me = lax.axis_index("tensor")
     f32 = jnp.float32
     bf16 = jnp.bfloat16
-    total = pos_ref.shape[0]
+    total = (1 + STEPS) * count
     group = H // KVH
     q_dev, kv_dev = per_dev
 
@@ -216,7 +326,12 @@
         return all_ref[j // kv_dev, q_dev + j % kv_dev]
 
     scale = 1.0 / math.sqrt(HD)
-    positions = pos_ref[...]
+    row_ids = lax.broadcasted_iota(jnp.int32, (count, 1), 0)
+    lens = jnp.zeros((count, 1), jnp.int32)
+    for d in range(count):
+        lens = jnp.where(row_ids == d, lens_ref[d], lens)
+    offset = offset_ref[0]
+    positions = jnp.concatenate([offset + row_ids] + [lens + t for t in range(STEPS)], axis=0)
     cos_part = jnp.ones((total, HD), f32)
     sin_part = jnp.zeros((total, HD), f32)
     for bit in range(rotation_bits):
@@ -237,21 +352,18 @@
 
     prefix_dev = pk_ref.shape[0]
     slot = lax.broadcasted_iota(jnp.int32, (1, prefix_dev), 1)
-    prefix_seen = me * prefix_dev + slot < positions[0:1, :]
+    prefix_seen = me * prefix_dev + slot < offset
 
     pool_dev = dk_ref.shape[0]
     block_dev = pool_dev // PAGE
     token = lax.broadcasted_iota(jnp.int32, (1, pool_dev), 1)
     block_of = me * block_dev + token // PAGE
-    entries = map_ref.shape[0]
-    entry = lax.broadcasted_iota(jnp.int32, (entries, 1), 0)
-    found = jnp.sum(jnp.where(map_ref[...] == block_of, entry, 0), axis=0, keepdims=True)
-    row_of = found // BLK_ROW
-    place = (found % BLK_ROW) * PAGE + token % PAGE
-    row_ids = lax.broadcasted_iota(jnp.int32, (count, 1), 0)
-    lens = positions[count : 2 * count, :]
-    length = jnp.sum(jnp.where(row_ids == row_of, lens, 0), axis=0, keepdims=True)
-    key_row = jnp.where(place < length, row_of, -1)
+    entry_of = jnp.zeros((count, pool_dev), jnp.int32)
+    for k in range(BLK_ROW):
+        entry_of = jnp.where(map_ref[:, k : k + 1] == block_of, k + 1, entry_of)
+    place = (entry_of - 1) * PAGE + token % PAGE
+    live = (entry_of > 0) & (place < lens)
+    key_row = jnp.sum(jnp.where(live, row_ids + 1, 0), axis=0, keepdims=True) - 1
 
     nh = heads_at_once
     span_q = lax.broadcasted_iota(jnp.int32, (nh * count, 1), 0) % count
@@ -276,8 +388,9 @@
         top = jnp.maximum(
             jnp.max(s1, axis=1, keepdims=True), jnp.max(s2, axis=1, keepdims=True)
         )
-        w1 = jnp.where(seen, jnp.exp(s1 - top), 0.0)
-        w2 = jnp.where(seen2, jnp.exp(s2 - top), 0.0)
+        top = jnp.maximum(top, top_floor)
+        w1 = jnp.exp(s1 - top)
+        w2 = jnp.exp(s2 - top)
         den = jnp.sum(w1, axis=1, keepdims=True) + jnp.sum(w2, axis=1, keepdims=True)
         num = jnp.dot(w1.astype(bf16), values, preferred_element_type=f32) + jnp.dot(
             w2.astype(bf16), values2, preferred_element_type=f32
@@ -357,7 +470,7 @@
     ]
     for copy in locals_:
         copy.start()
-    greet(count, me)
+    greet_all(count, me)
 
     def remote(a, i):
         peer = lax.rem(me + i, count)
@@ -421,30 +534,18 @@
     rows_dev = decode_rows.shape[1]
     assert span_dev == 1 and rows_dev == 1
     kinds = 1 + STEPS
-    local_rows = jnp.concatenate([span_rows, decode_rows.reshape(STEPS, D)], axis=0)
-    normed = normalize(local_rows, norm_gain)
-    gathered = spread(normed.reshape(kinds * 16, D // 16), layout, 0)
-    shard_rows = gathered.reshape(count, kinds, D).transpose(1, 0, 2).reshape(kinds * count, D)
     total = kinds * count
-    queries = jnp.dot(shard_rows, w_query, preferred_element_type=jnp.float32).astype(jnp.bfloat16)
-    keyval = jnp.dot(shard_rows, w_keyval, preferred_element_type=jnp.float32).astype(jnp.bfloat16)
-
-    q_dev, kv_dev = queries.shape[1] // HD, keyval.shape[1] // HD
-    if queries.shape[1] % HD == 0 and keyval.shape[1] % HD == 0:
-        heads = jnp.concatenate([queries, keyval], axis=1).reshape(total, -1, HD)
-        heads = spread(heads.transpose(1, 0, 2), layout, 1)
+    cut, kv_cols = w_query.shape[1], w_keyval.shape[1]
+    heads = front(layout, span_rows, decode_rows, norm_gain, w_query, w_keyval)
+    if heads.ndim == 4:
+        q_dev, kv_dev = cut // HD, kv_cols // HD
     else:
-        cut = queries.shape[1]
-        heads = spread(jnp.concatenate([queries, keyval], axis=1), layout, 1).transpose(1, 0, 2)
+        heads = heads.transpose(1, 0, 2)
         heads = jnp.concatenate(
             [heads[:, :, :cut].reshape(total, -1, HD), heads[:, :, cut:].reshape(total, -1, HD)],
             axis=1,
         ).transpose(1, 0, 2)[None]
         q_dev, kv_dev = H, 2 * KVH
-    offset = span_offset[0]
-    positions = jnp.concatenate(
-        [offset + jnp.arange(count, dtype=jnp.int32)] + [context_lens + s for s in range(STEPS)]
-    )[:, None]
     cos_table, sin_table = rotation_tables(HD // 2)
     tile = lambda x: jnp.concatenate([x, x], axis=1)
     part, stat, cache = pl.pallas_call(
@@ -456,7 +557,9 @@
             jax.ShapeDtypeStruct((count * 8, 2 * H), jnp.float32),
             jax.ShapeDtypeStruct((2 * KVH, HD), jnp.float32),
         ],
-        in_specs=[VMEM_SPEC] * 9,
+        in_specs=[VMEM_SPEC] * 6
+        + [pl.BlockSpec(memory_space=pltpu.SMEM)] * 2
+        + [VMEM_SPEC] * 2,
         out_specs=[VMEM_SPEC] * 3,
         scratch_shapes=[
             pltpu.VMEM((total, HD), jnp.float32),
@@ -472,8 +575,9 @@
         prefix_values,
         pool_keys.reshape(-1, KVH * HD),
         pool_values.reshape(-1, KVH * HD),
-        row_blocks.reshape(-1, 1),
-        positions,
+        row_blocks,
+        span_offset,
+        context_lens,
         tile(cos_table),
         tile(sin_table),
     )

time: 93.9 us -> 75.1 us (0.80)
  matrix products: 5.4 us -> 0 us
  local copies, waits for them, and re-layouts: 10 us -> 4.71 us
  other arithmetic: 5.26 us -> 0.7 us
  Pallas kernels: 71 us -> 67.9 us
    dot_general x2 -> x0, matrix products: 5.4 us -> none  [the longest x1 4.91 us: shards(): jnp.dot(shard_rows, w_query, preferred_element_type=jnp.float32)]
    reshape x2 -> x1, local copies, waits for them, and re-layouts: 4.41 us -> 1.35 us  [front(): norm_gain.reshape(1, depth)]
    pallas_call x2 -> x1, Pallas kernels: 32 us -> 29.5 us  [front(): pl.pallas_call(functools.partial(front_kernel, layout), out_shape=jax.Sha...]
    convert_element_type x2 -> x0, other arithmetic: 1.53 us -> none  [the longest x1 0.84 us: normalize(): widened = row_block.astype(jnp.float32)]
    reduce_sum x1 -> x0, other arithmetic: 0.98 us -> none  [normalize(): mean_square = jnp.mean(widened * widened, axis=-1, keepdims=True)]
    unnamed x5 -> x3, local copies, waits for them, and re-layouts: 1.97 us -> 1.96 us
where the time goes in v3:
time: 75.1 us; the launch traced here: 74.6 us
  Pallas kernels  67.9 us (90%)
  local copies, waits for them, and re-layouts  4.71 us (6%)
  between operations  1.3 us (2%)
    pallas_call x1, Pallas kernels, front(): pl.pallas_call(functools.partial(front_kernel, layout), out_shape=jax.Sha...  29.5 us
    pallas_call x1, Pallas kernels, shards(): pl.pallas_call(functools.partial(merge_kernel, count), out_shape=jax.Shap...  26.1 us
    pallas_call x1, Pallas kernels, shards(): pl.pallas_call(functools.partial(attend_kernel, count, H // KVH if count...  12.3 us
    unnamed x3, local copies, waits for them, and re-layouts  1.96 us

profile of v3, /device:TPU:13, one launch (start us, length us, event | category | flops | bytes accessed | tf_op | source)
XLA Modules:
  0.0 74.6 jit_solution(13211450436016095765)
XLA Ops:
  1.3 1.4 %reshape.39.gain_ref = bf16[1,8192]{1,0:T(2,128)(2,1)} reshape(bf16[8192]{0:T(1024)(128)(2,1)} %param.16) | data formatting | bytes 32768 | tf_op jit(solution)/shard_map/reshape | solution.py:290
  2.6 29.5 %front.1.all_ref = bf16[16,5,48,128]{3,2,1,0:T(8,128)(2,1)} custom-call(bf16[1,8192]{1,0:T(2,128)(2,1)} %span_ref.1, bf16[2,8192]{1,0:T(2,128)(2,1)} %bitcast.18, bf16[1,8192]{1,0:T(2,128)(2,1)} %reshape.39.gain_ref, bf16[8192,512]{1,0:T(8,128)(2,1)} %wq_hbm.1, bf16[8192,128]{1,0:T(8,128)(2,1)} %wkv_hbm.1), custom_call_target="tpu_custom_call" | custom-call | tf_op jit(solution)/shard_map/front/pallas_call | solution.py:269
  32.1 12.3 %attend.1 = (bf16[16,192,128]{2,1,0:T(8,128)(2,1)}, f32[128,128]{1,0:T(8,128)}, f32[16,128]{1,0:T(8,128)}) custom-call(bf16[16,5,48,128]{3,2,1,0:T(8,128)(2,1)} %front.1.all_ref, bf16[256,1024]{1,0:T(8,128)(2,1)} %pk_ref.1, bf16[256,1024]{1,0:T(8,128)(2,1)} %pv_ref.1, bf16[512,1024]{1,0:T(8,128)(2,1)} %bitcast.15, bf16[512,1024]{1,0:T(8,128)(2,1)} %bitcast.16, ...), custom_call_target="tpu_custom_call" | custom-call | tf_op jit(solution)/shard_map/attend/pallas_call | solution.py:551
  44.4 26.1 %merge.1 = bf16[3,64,128]{2,1,0:T(8,128)(2,1)} custom-call(bf16[16,192,128]{2,1,0:T(8,128)(2,1)} %get-tuple-element.6.part_ref, f32[16,8,128]{2,1,0:T(8,128)} %bitcast.17), custom_call_target="tpu_custom_call" | custom-call | tf_op jit(solution)/shard_map/merge/pallas_call | solution.py:584
  70.5 0.7 convert_bitcast_fusion
  71.2 0.6 copy.22
  71.9 0.7 slice_bitcast_fusion
  72.6 0.8 %slice.7 = bf16[2,64,128]{2,1,0:T(8,128)(2,1)S(1)} slice(bf16[3,64,128]{2,1,0:T(8,128)(2,1)} %merge.1), slice={[1:3], [0:64], [0:128]} | slice | bytes 65536 | tf_op jit(solution)/shard_map/slice | solution.py:602
  73.3 0.6 reshape.43
  74.0 0.6 copy.21

commit v4 on v3

--- a/solution.py
+++ b/solution.py
@@ -59,7 +59,6 @@
         return carry
 
     lax.fori_loop(1, count, signal, 0)
-    pl.semaphore_wait(barrier, count - 1)
 
 
 def greet_near(layout):
@@ -304,15 +303,24 @@
     lens_ref,
     cos_ref,
     sin_ref,
-    part_ref,
-    stat_ref,
-    cache_ref,
+    span_out,
+    decode_out,
+    cache_out,
     turn_cos,
     turn_sin,
     wide,
     stats,
+    cache_ref,
+    own_parts,
+    own_stats,
+    parts,
+    all_stats,
+    send_sems,
+    recv_sems,
+    local_sems,
 ):
     me = lax.axis_index("tensor")
+    greet_all(count, me)
     f32 = jnp.float32
     bf16 = jnp.bfloat16
     total = (1 + STEPS) * count
@@ -377,7 +385,7 @@
     pick = lax.broadcasted_iota(jnp.int32, (count, 1), 0) == me
     stat_lane = lax.broadcasted_iota(jnp.int32, (count, 2 * H), 1)
     stats[...] = jnp.zeros_like(stats)
-    stat_ref[...] = jnp.zeros_like(stat_ref)
+    own_stats[...] = jnp.zeros_like(own_stats)
     across = (((1,), (1,)), ((), ()))
 
     def soft(q, keys, values, seen, keys2, values2, seen2):
@@ -396,6 +404,42 @@
             w2.astype(bf16), values2, preferred_element_type=f32
         )
         return top, den, num
+
+    kinds = 1 + STEPS
+
+    def part_copy(i, g):
+        peer = lax.rem(me + i, count)
+        return pltpu.make_async_remote_copy(
+            src_ref=own_parts.at[peer, g],
+            dst_ref=parts.at[me, g],
+            send_sem=send_sems.at[0, i],
+            recv_sem=recv_sems.at[0, i],
+            device_id={"tensor": peer},
+            device_id_type=pl.DeviceIdType.MESH,
+        )
+
+    def all_parts(i):
+        return pltpu.make_async_remote_copy(
+            src_ref=own_parts.at[lax.rem(me + i, count)],
+            dst_ref=parts.at[lax.rem(me + count - i, count)],
+            send_sem=send_sems.at[0, i],
+            recv_sem=recv_sems.at[0, i],
+            device_id={"tensor": lax.rem(me + i, count)},
+            device_id_type=pl.DeviceIdType.MESH,
+        )
+
+    def stat_copy(i):
+        peer = lax.rem(me + i, count)
+        return pltpu.make_async_remote_copy(
+            src_ref=own_stats.at[pl.ds(pl.multiple_of(peer * 8, 8), 8)],
+            dst_ref=all_stats.at[me],
+            send_sem=send_sems.at[1, i],
+            recv_sem=recv_sems.at[1, i],
+            device_id={"tensor": peer},
+            device_id_type=pl.DeviceIdType.MESH,
+        )
+
+    pl.semaphore_wait(pltpu.get_barrier_semaphore(), count - 1)
 
     def per_head(g, carry):
         cols = pl.ds(pl.multiple_of(g * HD, HD), HD)
@@ -439,79 +483,75 @@
                         at = (i * STEPS + kind - 1) * count
                         rows = slice(at, at + count)
                         top, den, num = dec_top[rows], dec_den[rows], dec_num[rows]
-                    wide[kind, pl.ds(head, count, stride=H), :] = num
+                    wide[pl.ds(kind * group + first + i, count, stride=kinds * group), :] = num
                     stats[kind] = jnp.where(
                         stat_lane == head,
                         top,
                         jnp.where(stat_lane == H + head, den, stats[kind]),
                     )
+
+        def pack(d, carry):
+            rows = pl.ds(pl.multiple_of(d * kinds * group, kinds * group), kinds * group)
+            own_parts[d, g] = wide[rows, :].astype(bf16)
+            return carry
+
+        def send(i, carry):
+            part_copy(i, g).start()
+            return carry
+
+        lax.fori_loop(0, count, pack, 0)
+        lax.fori_loop(1, count, send, 0)
         return carry
 
     lax.fori_loop(0, KVH, per_head, 0)
-    for kind in range(1 + STEPS):
-        stat_ref[pl.ds(kind, count, stride=8), :] = stats[kind]
-
-    def pack(d, carry):
-        for kind in range(1 + STEPS):
-            rows = pl.ds(pl.multiple_of(d * H, H), H)
-            part_ref[d, kind * H : (kind + 1) * H, :] = wide[kind, rows, :].astype(bf16)
+    for kind in range(kinds):
+        own_stats[pl.ds(kind, count, stride=8), :] = stats[kind]
+
+    def send_stats(i, carry):
+        stat_copy(i).start()
         return carry
 
-    lax.fori_loop(0, count, pack, 0)
-
-
-def merge_kernel(count, part_ref, stat_ref, out_ref, parts, stats, send_sems, recv_sems, local_sems):
-    me = lax.axis_index("tensor")
-    f32 = jnp.float32
-    sources, targets = (part_ref, stat_ref), (parts, stats)
-    locals_ = [
-        pltpu.make_async_copy(sources[a].at[me], targets[a].at[me], local_sems.at[a])
-        for a in range(2)
-    ]
-    for copy in locals_:
+    lax.fori_loop(1, count, send_stats, 0)
+    own = (
+        pltpu.make_async_copy(own_parts.at[me], parts.at[me], local_sems.at[0]),
+        pltpu.make_async_copy(
+            own_stats.at[pl.ds(pl.multiple_of(me * 8, 8), 8)], all_stats.at[me], local_sems.at[1]
+        ),
+    )
+    for copy in own:
         copy.start()
-    greet_all(count, me)
-
-    def remote(a, i):
-        peer = lax.rem(me + i, count)
-        return pltpu.make_async_remote_copy(
-            src_ref=sources[a].at[peer],
-            dst_ref=targets[a].at[me],
-            send_sem=send_sems.at[a, i],
-            recv_sem=recv_sems.at[a, i],
-            device_id={"tensor": peer},
-            device_id_type=pl.DeviceIdType.MESH,
-        )
-
-    def start(i, carry):
-        for a in range(2):
-            remote(a, i).start()
+    for j in range(2 * KVH):
+        cache_out[0:1, j * HD : (j + 1) * HD] = cache_ref[j : j + 1, :].astype(cache_out.dtype)
+    for copy in own:
+        copy.wait()
+
+    def finish(i, carry):
+        all_parts(i).wait()
+        stat_copy(i).wait()
         return carry
 
-    def finish(i, carry):
-        for a in range(2):
-            remote(a, i).wait()
-        return carry
-
-    lax.fori_loop(1, count, start, 0)
-    for copy in locals_:
-        copy.wait()
     lax.fori_loop(1, count, finish, 0)
-    top = stats[0]
+    best = all_stats[0]
     for d in range(1, count):
-        top = jnp.maximum(top, stats[d])
-    den = jnp.zeros_like(top)
+        best = jnp.maximum(best, all_stats[d])
+    den = jnp.zeros_like(best)
     for d in range(count):
-        den = den + jnp.exp(stats[d] - top) * pltpu.roll(stats[d], H, 1)
+        den = den + jnp.exp(all_stats[d] - best) * pltpu.roll(all_stats[d], H, 1)
     inverse = 1.0 / den
-    share = jnp.concatenate([jnp.exp(stats[d] - top) * inverse for d in range(count)], axis=0).T
-    for kind in range(1 + STEPS):
-        acc = jnp.zeros((H, HD), f32)
-        for d in range(count):
-            acc = acc + share[:H, d * 8 + kind : d * 8 + kind + 1] * parts[
-                d, kind * H : (kind + 1) * H, :
-            ].astype(f32)
-        out_ref[kind] = acc.astype(out_ref.dtype)
+    share = jnp.concatenate(
+        [jnp.exp(all_stats[d] - best) * inverse for d in range(count)], axis=0
+    ).T
+    sums = [jnp.zeros((H, HD), f32) for _ in range(kinds)]
+    for d in range(count):
+        arrived = parts[d].astype(f32)
+        for kind in range(kinds):
+            rows = arrived[:, kind * group : (kind + 1) * group, :].reshape(H, HD)
+            sums[kind] = sums[kind] + share[:H, d * 8 + kind : d * 8 + kind + 1] * rows
+    for h in range(H):
+        cols = slice(h * HD, (h + 1) * HD)
+        span_out[0:1, cols] = sums[0][h : h + 1, :].astype(span_out.dtype)
+        for t in range(STEPS):
+            decode_out[t : t + 1, cols] = sums[1 + t][h : h + 1, :].astype(decode_out.dtype)
 
 
 def shards(
@@ -548,14 +588,15 @@
         q_dev, kv_dev = H, 2 * KVH
     cos_table, sin_table = rotation_tables(HD // 2)
     tile = lambda x: jnp.concatenate([x, x], axis=1)
-    part, stat, cache = pl.pallas_call(
+    dma = pltpu.SemaphoreType.DMA
+    span_attended, decode_attended, span_cache = pl.pallas_call(
         functools.partial(
             attend_kernel, count, H // KVH if count <= 32 else 1, (q_dev, kv_dev)
         ),
         out_shape=[
-            jax.ShapeDtypeStruct((count, kinds * H, HD), jnp.bfloat16),
-            jax.ShapeDtypeStruct((count * 8, 2 * H), jnp.float32),
-            jax.ShapeDtypeStruct((2 * KVH, HD), jnp.float32),
+            jax.ShapeDtypeStruct((1, D), jnp.bfloat16),
+            jax.ShapeDtypeStruct((STEPS, D), jnp.bfloat16),
+            jax.ShapeDtypeStruct((1, 2 * KVH * HD), jnp.bfloat16),
         ],
         in_specs=[VMEM_SPEC] * 6
         + [pl.BlockSpec(memory_space=pltpu.SMEM)] * 2
@@ -564,10 +605,20 @@
         scratch_shapes=[
             pltpu.VMEM((total, HD), jnp.float32),
             pltpu.VMEM((total, HD), jnp.float32),
-            pltpu.VMEM((kinds, count * H, HD), jnp.float32),
+            pltpu.VMEM((count * kinds * H // KVH, HD), jnp.float32),
             pltpu.VMEM((kinds, count, 2 * H), jnp.float32),
+            pltpu.VMEM((2 * KVH, HD), jnp.float32),
+            pltpu.VMEM((count, KVH, kinds * H // KVH, HD), jnp.bfloat16),
+            pltpu.VMEM((count * 8, 2 * H), jnp.float32),
+            pltpu.VMEM((count, KVH, kinds * H // KVH, HD), jnp.bfloat16),
+            pltpu.VMEM((count, 8, 2 * H), jnp.float32),
+            dma((2, count)),
+            dma((2, count)),
+            dma((2,)),
         ],
-        compiler_params=pltpu.CompilerParams(vmem_limit_bytes=VMEM_BYTES),
+        compiler_params=pltpu.CompilerParams(
+            collective_id=1, has_side_effects=True, vmem_limit_bytes=VMEM_BYTES
+        ),
         name="attend",
     )(
         heads,
@@ -581,26 +632,7 @@
         tile(cos_table),
         tile(sin_table),
     )
-    merged = pl.pallas_call(
-        functools.partial(merge_kernel, count),
-        out_shape=jax.ShapeDtypeStruct((kinds, H, HD), jnp.bfloat16),
-        in_specs=[VMEM_SPEC] * 2,
-        out_specs=VMEM_SPEC,
-        scratch_shapes=[
-            pltpu.VMEM((count, kinds * H, HD), jnp.bfloat16),
-            pltpu.VMEM((count, 8, 2 * H), jnp.float32),
-            pltpu.SemaphoreType.DMA((2, count)),
-            pltpu.SemaphoreType.DMA((2, count)),
-            pltpu.SemaphoreType.DMA((2,)),
-        ],
-        compiler_params=pltpu.CompilerParams(
-            collective_id=2, has_side_effects=True, vmem_limit_bytes=VMEM_BYTES
-        ),
-        name="merge",
-    )(part, stat.reshape(count, 8, 2 * H))
-    span_attended = merged[0].reshape(1, D)
-    decode_attended = merged[1:].reshape(STEPS, 1, D)
-    span_cache = cache.reshape(1, 2 * KVH * HD).astype(jnp.bfloat16)
+    decode_attended = decode_attended.reshape(STEPS, 1, D)
     return (span_attended, decode_attended, span_cache)
 
 

time: 75.1 us -> 67.3 us (0.90)
  the two profiles are of different devices: /device:TPU:13 before, /device:TPU:0 now
where the time goes in v4:
time: 67.3 us; the launch traced here: 66.9 us
  Pallas kernels  60.2 us (89%)
  local copies, waits for them, and re-layouts  5.46 us (8%)
  between operations  1.29 us (2%)
    pallas_call x1, Pallas kernels, front(): pl.pallas_call(functools.partial(front_kernel, layout), out_shape=jax.Sha...  31.1 us
    pallas_call x1, Pallas kernels, shards(): pl.pallas_call(functools.partial(attend_kernel, count, H // KVH if count...  29.1 us
    unnamed x3, local copies, waits for them, and re-layouts  4.1 us
    reshape x1, local copies, waits for them, and re-layouts, front(): norm_gain.reshape(1, depth)  1.35 us

profile of v4, /device:TPU:0, one launch (start us, length us, event | category | flops | bytes accessed | tf_op | source)
XLA Modules:
  0.0 66.9 jit_solution(16570222273699648391)
XLA Ops:
  1.3 1.4 %reshape.22.gain_ref = bf16[1,8192]{1,0:T(2,128)(2,1)} reshape(bf16[8192]{0:T(1024)(128)(2,1)} %param.16) | data formatting | bytes 32768 | tf_op jit(solution)/shard_map/reshape | solution.py:289
  2.6 31.1 %front.1.all_ref = bf16[16,5,48,128]{3,2,1,0:T(8,128)(2,1)} custom-call(bf16[1,8192]{1,0:T(2,128)(2,1)} %span_ref.1, bf16[2,8192]{1,0:T(2,128)(2,1)} %bitcast.6, bf16[1,8192]{1,0:T(2,128)(2,1)} %reshape.22.gain_ref, bf16[8192,512]{1,0:T(8,128)(2,1)} %wq_hbm.1, bf16[8192,128]{1,0:T(8,128)(2,1)} %wkv_hbm.1), custom_call_target="tpu_custom_call" | custom-call | tf_op jit(solution)/shard_map/front/pallas_call | solution.py:268
  33.7 29.1 %attend.1 = (bf16[1,8192]{1,0:T(2,128)(2,1)}, bf16[2,8192]{1,0:T(2,128)(2,1)}, bf16[1,2048]{1,0:T(2,128)(2,1)}) custom-call(bf16[16,5,48,128]{3,2,1,0:T(8,128)(2,1)} %front.1.all_ref, bf16[256,1024]{1,0:T(8,128)(2,1)} %pk_ref.1, bf16[256,1024]{1,0:T(8,128)(2,1)} %pv_ref.1, bf16[512,1024]{1,0:T(8,128)(2,1)} %bitcast.4, bf16[512,1024]{1,0:T(8,128)(2,1)} %bitcast.5, ...), custom_call_target="tpu_custom_call" | custom-call | tf_op jit(solution)/shard_map/attend/pallas_call | solution.py:592
  62.8 1.4 %copy.21 = bf16[1,8192]{1,0:T(2,128)(2,1)} copy(bf16[1,8192]{1,0:T(2,128)(2,1)} %get-tuple-element.12) | data formatting | bytes 32768
  64.2 1.4 %copy.22 = bf16[2,1,8192]{2,0,1:T(2,128)(2,1)} copy(bf16[2,1,8192]{2,0,1:T(2,128)(2,1)} %bitcast.7) | data formatting | bytes 65536
  65.6 1.3 %copy.23 = bf16[1,2048]{1,0:T(2,128)(2,1)} copy(bf16[1,2048]{1,0:T(2,128)(2,1)} %get-tuple-element.14) | data formatting | bytes 8192

commit v5 on v4

--- a/solution.py
+++ b/solution.py
@@ -131,9 +131,10 @@
         ).wait_recv()
 
     slots = iter(range(outer * inner * cores))
-    for i in range(1, outer):
+    near = sorted(range(outer), key=lambda i: min(i, outer - i))
+    for i in near[1:]:
         send(me, source, index(lax.rem(plane + i, outer), column, core), next(slots))
-    for j in range(outer):
+    for j in near:
         owner = index(lax.rem(plane + outer - j, outer), column, core)
         if j > 0:
             arrived(owner)
@@ -142,7 +143,7 @@
             send(owner, src, index(plane, lax.rem(column + k, inner), core), next(slots))
         for k in range(1, cores):
             send(owner, src, index(plane, column, lax.rem(core + k, cores)), next(slots))
-    for j in range(outer):
+    for j in near:
         for k in range(1, inner):
             owner = index(
                 lax.rem(plane + outer - j, outer), lax.rem(column + inner - k, inner), core
@@ -196,7 +197,7 @@
             copy = pltpu.make_async_copy(src.at[rows], dst.at[rows], weight_sems.at[a, i])
             copy.start()
             fetches.append(copy)
-    gain = gain_ref[...].astype(f32)
+    gain = gain_ref[...].astype(f32).reshape(1, depth)
     width = lines.shape[1]
     folds = depth // width
     kinds = lines.shape[0] // folds
@@ -286,7 +287,7 @@
             collective_id=0, has_side_effects=True, vmem_limit_bytes=VMEM_BYTES
         ),
         name="front",
-    )(span_rows, decode_rows.reshape(STEPS, depth), norm_gain.reshape(1, depth), w_query, w_keyval)
+    )(span_rows, decode_rows.reshape(STEPS, depth), norm_gain, w_query, w_keyval)
 
 
 def attend_kernel(
@@ -594,9 +595,9 @@
             attend_kernel, count, H // KVH if count <= 32 else 1, (q_dev, kv_dev)
         ),
         out_shape=[
-            jax.ShapeDtypeStruct((1, D), jnp.bfloat16),
-            jax.ShapeDtypeStruct((STEPS, D), jnp.bfloat16),
-            jax.ShapeDtypeStruct((1, 2 * KVH * HD), jnp.bfloat16),
+            jax.ShapeDtypeStruct((1, D), jnp.float32),
+            jax.ShapeDtypeStruct((STEPS, D), jnp.float32),
+            jax.ShapeDtypeStruct((1, 2 * KVH * HD), jnp.float32),
         ],
         in_specs=[VMEM_SPEC] * 6
         + [pl.BlockSpec(memory_space=pltpu.SMEM)] * 2
@@ -633,7 +634,7 @@
         tile(sin_table),
     )
     decode_attended = decode_attended.reshape(STEPS, 1, D)
-    return (span_attended, decode_attended, span_cache)
+    return tuple(x.astype(jnp.bfloat16) for x in (span_attended, decode_attended, span_cache))
 
 
 def solution(mesh):

time: 67.3 us -> 65 us (0.966)
  local copies, waits for them, and re-layouts: 5.46 us -> 0 us
  other arithmetic: 0 us -> 4.17 us
  Pallas kernels: 60.2 us -> 59.2 us
    convert_element_type x0 -> x3, other arithmetic: none -> 4.17 us  [shards(): x.astype(jnp.bfloat16)]
    unnamed x3 -> x0, local copies, waits for them, and re-layouts: 4.1 us -> none
    reshape x1 -> x0, local copies, waits for them, and re-layouts: 1.35 us -> none  [front(): norm_gain.reshape(1, depth)]
    pallas_call x1, Pallas kernels: 29.1 us -> 28.2 us  [shards(): pl.pallas_call(functools.partial(attend_kernel, count, H // KVH if count...]
where the time goes in v5:
time: 65 us; the launch traced here: 64.7 us
  Pallas kernels  59.2 us (91%)
  other arithmetic  4.17 us (6%)
  between operations  1.3 us (2%)
    pallas_call x1, Pallas kernels, front(): pl.pallas_call(functools.partial(front_kernel, layout), out_shape=jax.Sha...  31 us
    pallas_call x1, Pallas kernels, shards(): pl.pallas_call(functools.partial(attend_kernel, count, H // KVH if count...  28.2 us
    convert_element_type x3, other arithmetic, shards(): x.astype(jnp.bfloat16)  4.17 us

profile of v5, /device:TPU:0, one launch (start us, length us, event | category | flops | bytes accessed | tf_op | source)
XLA Modules:
  0.0 64.7 jit_solution(1152166928311670919)
XLA Ops:
  1.3 31.0 %front.1.all_ref = bf16[16,5,48,128]{3,2,1,0:T(8,128)(2,1)} custom-call(bf16[1,8192]{1,0:T(2,128)(2,1)} %span_ref.1, bf16[2,8192]{1,0:T(2,128)(2,1)} %bitcast.7, bf16[8192]{0:T(1024)(128)(2,1)} %gain_ref.1, bf16[8192,512]{1,0:T(8,128)(2,1)} %wq_hbm.1, bf16[8192,128]{1,0:T(8,128)(2,1)} %wkv_hbm.1), custom_call_target="tpu_custom_call" | custom-call | tf_op jit(solution)/shard_map/front/pallas_call | solution.py:269
  32.2 28.2 %attend.1 = (f32[1,8192]{1,0:T(1,128)}, f32[2,8192]{1,0:T(2,128)}, f32[1,2048]{1,0:T(1,128)}) custom-call(bf16[16,5,48,128]{3,2,1,0:T(8,128)(2,1)} %front.1.all_ref, bf16[256,1024]{1,0:T(8,128)(2,1)} %pk_ref.1, bf16[256,1024]{1,0:T(8,128)(2,1)} %pv_ref.1, bf16[512,1024]{1,0:T(8,128)(2,1)} %bitcast.5, bf16[512,1024]{1,0:T(8,128)(2,1)} %bitcast.6, ...), custom_call_target="tpu_custom_call" | custom-call | tf_op jit(solution)/shard_map/attend/pallas_call | solution.py:593
  60.5 1.4 %convert_element_type.12 = bf16[1,8192]{1,0:T(2,128)(2,1)} convert(f32[1,8192]{1,0:T(1,128)} %get-tuple-element.6) | non-fusion elementwise | flops 8192 | bytes 49152 | tf_op jit(solution)/shard_map/convert_element_type | solution.py:637
  61.9 1.3 %convert_element_type.15 = bf16[1,2048]{1,0:T(2,128)(2,1)} convert(f32[1,2048]{1,0:T(1,128)} %get-tuple-element.8) | non-fusion elementwise | flops 2048 | bytes 12288 | tf_op jit(solution)/shard_map/convert_element_type | solution.py:637
  63.2 1.5 %convert_bitcast_fusion = bf16[2,1,8192]{2,0,1:T(2,128)(2,1)} fusion(f32[2,8192]{1,0:T(2,128)} %get-tuple-element.7), kind=kLoop, calls=%fused_computation | loop fusion | flops 16384 | bytes 98304 | tf_op jit(solution)/shard_map/convert_element_type | solution.py:637
